TPU v7x, 256 devices: a whole 4x4x8 slice. The times are simulated.
256 devices in a mesh: seq: 32 (over y, z), expert: 8 (over x, core).
Axes of the slice: x: 4, y: 4, z: 8, core: 2. Of those that a mesh axis runs over, the one named last changes fastest.
Arguments:
- grad_out: bfloat16 [32768, 2048], P(('seq', 'expert')), may hold values from -6 to 6
- expert_input: bfloat16 [32768, 2048], P(('seq', 'expert')), may hold values from -6 to 6
- expert_index: int32 [32768, 2], P(('seq', 'expert')), may hold values from 0 to 7, all different within a row; in each aligned block of 128 rows (0 to 127, 128 to 255, ...) at most 64 rows name the same one
- route_weight: float32 [32768, 2], P(('seq', 'expert')), may hold values from 0.1 to 1
- up_weight: bfloat16 [8, 2048, 768], P('expert'), may hold values from -0.125 to 0.125
- down_weight: bfloat16 [8, 768, 2048], P('expert'), may hold values from -0.21875 to 0.21875
- out_weight: bfloat16 [4096, 2048], P('expert'), may hold values from -0.125 to 0.125
- conv_value: bfloat16 [32768, 4096], P('seq', 'expert'), may hold values from -6 to 6
- conv_weight: float32 [4, 4096], P(None, 'expert'), may hold values from -3 to 3
- step_size: float32 [64, 32768], P('expert', 'seq'), may hold values from 0.25 to 1
- log_decay: float32 [64, 32768], P('expert', 'seq'), may hold values from -1 to 0
- skip_gain: float32 [64], P('expert'), may hold values from 0.2 to 0.6
- input_basis: bfloat16 [32768, 1024], P('seq', 'expert'), may hold values from -0.09375 to 0.09375
- output_basis: bfloat16 [32768, 1024], P('seq', 'expert'), may hold values from -0.09375 to 0.09375
Outputs:
- residual_grad: bfloat16 [32768, 2048], P(('seq', 'expert'))
- conv_grad: bfloat16 [32768, 4096], P('seq', 'expert')
- input_basis_grad: bfloat16 [32768, 1024], P('seq', 'expert')
- output_basis_grad: bfloat16 [32768, 1024], P('seq', 'expert')
Inputs may be any that keep to these rules, and one draw needn't show every extreme that they name: `expert_index`: in each aligned block of 128 rows (the rows of one device), no expert is named by more than 64 rows, and the 2 experts of a row differ.
All inputs are finite; a program needn't handle non-finite values.
Results may differ from a plain program's by a relative error of at most 0.01.
Values may be sent and summed in bfloat16 or wider, within the bound.
A program may use at most 128 MiB of HBM per device.

v0:
```python
import jax
import jax.numpy as jnp
from jax import lax
from jax.sharding import PartitionSpec as P

P_SIZE = 64
N = 128
KW = 4
SPAN = 128


def from_behind(value, axis, by):
    devices = lax.axis_size(axis)
    pairs = [(i, i + by) for i in range(devices) if 0 <= i + by < devices]
    return lax.ppermute(value, axis, pairs)


def slot_tables(block_index, block_weight, expert_count, capacity):
    flat_index = block_index.reshape(-1)
    onehot_table = (
        flat_index[:, None] == jnp.arange(expert_count, dtype=jnp.int32)[None, :]
    ).astype(jnp.int32)
    earlier_count = jnp.cumsum(onehot_table, axis=0) - onehot_table
    slot_rank = jnp.sum(earlier_count * onehot_table, axis=1)
    slot_place = flat_index * capacity + slot_rank
    owner_row = jnp.arange(flat_index.shape[0], dtype=jnp.int32) // block_index.shape[1]
    slot_match = (
        slot_place[:, None] == jnp.arange(expert_count * capacity, dtype=jnp.int32)[None, :]
    )
    source_row = jnp.sum(jnp.where(slot_match, owner_row[:, None], 0), axis=0)
    slot_filled = jnp.any(slot_match, axis=0)
    slot_weight = jnp.sum(jnp.where(slot_match, block_weight.reshape(-1)[:, None], 0.0), axis=0)
    return (slot_place, source_row, slot_filled, slot_weight)


def expert_rows(input_rows, grad_rows, up_matrix, down_matrix):
    hidden_pre = jnp.dot(input_rows, up_matrix, preferred_element_type=jnp.float32)
    hidden_back = jnp.dot(grad_rows, down_matrix.T, preferred_element_type=jnp.float32)
    inner_grad = (2.0 * jnp.maximum(hidden_pre, 0.0) * hidden_back).astype(jnp.bfloat16)
    return jnp.dot(inner_grad, up_matrix.T, preferred_element_type=jnp.float32).astype(jnp.bfloat16)


def combine_rows(grad_rows, slot_place, returned):
    row_count = grad_rows.shape[0]
    flat_rows = returned.reshape(-1, returned.shape[-1])
    picked = (
        jnp.take(flat_rows, slot_place, axis=0)
        .astype(jnp.float32)
        .reshape(row_count, -1, flat_rows.shape[-1])
    )
    return (grad_rows.astype(jnp.float32) + jnp.sum(picked, axis=1)).astype(jnp.bfloat16)


def silu_grad(values):
    sigmoid_value = jax.nn.sigmoid(values)
    return sigmoid_value + values * sigmoid_value * (1.0 - sigmoid_value)


def forward_terms(mixed_act, in_basis, step_blocks, decay_blocks):
    cumulative = jnp.cumsum(decay_blocks, axis=-1)
    in_scale = jnp.exp(cumulative[..., -1:] - cumulative) * step_blocks
    row_scale = jnp.transpose(in_scale, (2, 3, 0, 1))[..., None]
    mixed_weighted = (mixed_act.astype(jnp.float32) * row_scale).astype(jnp.bfloat16)
    local_end = jnp.einsum(
        "kqgn,kqghp->ghknp", in_basis, mixed_weighted, preferred_element_type=jnp.float32
    )
    return (cumulative, in_scale, mixed_weighted, local_end, jnp.exp(cumulative[..., -1]))


def backward_terms(cumulative, out_grad, out_basis):
    row_scale = jnp.transpose(jnp.exp(cumulative), (2, 3, 0, 1))[..., None]
    grad_weighted = (out_grad.astype(jnp.float32) * row_scale).astype(jnp.bfloat16)
    local_start = jnp.einsum(
        "kqgn,kqghp->ghknp", out_basis, grad_weighted, preferred_element_type=jnp.float32
    )
    return (grad_weighted, local_start)


def advance(state_now, pair_now):
    return (pair_now[0][..., None, None] * state_now + pair_now[1], state_now)


def chain_forward(block_decay, local_terms, initial):
    moved = (jnp.moveaxis(block_decay, 2, 0), jnp.moveaxis(local_terms, 2, 0))
    final, entering = lax.scan(advance, initial, moved)
    return (final, jnp.moveaxis(entering, 0, 2))


def chain_backward(block_decay, local_terms, initial):
    moved = (jnp.moveaxis(block_decay, 2, 0), jnp.moveaxis(local_terms, 2, 0))
    final, leaving = lax.scan(advance, initial, moved, reverse=True)
    return (final, jnp.moveaxis(leaving, 0, 2))


def block_grads(
    cumulative,
    in_scale,
    mixed_act,
    out_grad,
    in_basis,
    out_basis,
    mixed_weighted,
    grad_weighted,
    entering,
    leaving,
    step_blocks,
    skip_heads,
):
    block_len = cumulative.shape[-1]
    lower_mask = jnp.arange(block_len)[:, None] >= jnp.arange(block_len)[None, :]
    spread = jnp.where(lower_mask, cumulative[..., :, None] - cumulative[..., None, :], 0.0)
    decay_mask = jnp.where(lower_mask, jnp.exp(spread), 0.0)
    step_column = step_blocks[..., None, :]
    scores = jnp.einsum("kagn,kbgn->gkab", out_basis, in_basis, preferred_element_type=jnp.float32)
    weight_scores = (decay_mask * step_column * scores[:, None]).astype(jnp.bfloat16)
    grad_mixed = jnp.einsum(
        "kaghp,kbghp->ghkab", out_grad, mixed_act, preferred_element_type=jnp.float32
    )
    weight_grad = (decay_mask * step_column * grad_mixed).astype(jnp.bfloat16)
    entering_low = entering.astype(jnp.bfloat16)
    leaving_low = leaving.astype(jnp.bfloat16)
    inner_term = jnp.einsum(
        "ghkab,kaghp->kbghp", weight_scores, out_grad, preferred_element_type=jnp.float32
    )
    carried = jnp.einsum(
        "kbgn,ghknp->kbghp", in_basis, leaving_low, preferred_element_type=jnp.float32
    )
    row_scale = jnp.transpose(in_scale, (2, 3, 0, 1))[..., None]
    mixed_grad = (
        inner_term
        + row_scale * carried
        + skip_heads[None, None, :, :, None] * out_grad.astype(jnp.float32)
    )
    in_basis_grad = jnp.einsum(
        "ghkab,kagn->kbgn", weight_grad, out_basis, preferred_element_type=jnp.float32
    )
    in_basis_grad = in_basis_grad + jnp.einsum(
        "kbghp,ghknp->kbgn", mixed_weighted, leaving_low, preferred_element_type=jnp.float32
    )
    out_basis_grad = jnp.einsum(
        "kaghp,ghknp->kagn", grad_weighted, entering_low, preferred_element_type=jnp.float32
    )
    out_basis_grad = out_basis_grad + jnp.einsum(
        "ghkab,kbgn->kagn", weight_grad, in_basis, preferred_element_type=jnp.float32
    )
    return (mixed_grad, in_basis_grad, out_basis_grad)


def filter_back(value_grad, filter_taps, after_rows):
    row_count = value_grad.shape[0]
    padded = jnp.concatenate([value_grad, after_rows], axis=0)
    summed = filter_taps[0] * value_grad
    for tap_index in range(1, filter_taps.shape[0]):
        summed = summed + filter_taps[tap_index] * padded[tap_index : tap_index + row_count]
    return summed


def shards(
    grad_out,
    expert_input,
    expert_index,
    route_weight,
    up_weight,
    down_weight,
    out_weight,
    conv_value,
    conv_weight,
    step_size,
    log_decay,
    skip_gain,
    input_basis,
    output_basis,
):
    expert_count = lax.axis_size("expert")
    row_count, choose_count = expert_index.shape
    capacity = 2 * row_count * choose_count // expert_count
    model_width = grad_out.shape[1]
    head_count, seq_length = step_size.shape
    group_count = input_basis.shape[1] // N
    per_group = head_count // group_count
    block_count = seq_length // SPAN
    pre_value = conv_value.astype(jnp.float32)
    mixed_act = (
        jax.nn.silu(pre_value)
        .astype(jnp.bfloat16)
        .reshape(block_count, SPAN, group_count, per_group, P_SIZE)
    )
    in_basis = input_basis.reshape(block_count, SPAN, group_count, N)
    out_basis = output_basis.reshape(block_count, SPAN, group_count, N)
    step_blocks = step_size.reshape(group_count, per_group, block_count, SPAN)
    decay_blocks = log_decay.reshape(group_count, per_group, block_count, SPAN)
    skip_heads = skip_gain.reshape(group_count, per_group)
    cumulative, in_scale, mixed_weighted, local_end, block_decay = forward_terms(
        mixed_act, in_basis, step_blocks, decay_blocks
    )
    zero_state = jnp.zeros((group_count, per_group, N, P_SIZE), jnp.float32)
    device_decay = jnp.exp(jnp.sum(cumulative[..., -1], axis=-1))
    device_state, _ = chain_forward(block_decay, local_end, zero_state)

    def forward_turn(turn_index, incoming):
        return from_behind(
            (device_decay[..., None, None] * incoming + device_state).astype(jnp.bfloat16), "seq", 1
        ).astype(jnp.float32)

    enter_state = lax.fori_loop(0, lax.axis_size("seq") - 1, forward_turn, zero_state)
    _, entering = chain_forward(block_decay, local_end, enter_state)
    slot_place, source_row, slot_filled, slot_weight = slot_tables(
        expert_index, route_weight, expert_count, capacity
    )
    send_inputs = jnp.where(
        slot_filled[:, None],
        jnp.take(expert_input, source_row, axis=0),
        jnp.zeros((), expert_input.dtype),
    )
    send_grads = (
        jnp.take(grad_out, source_row, axis=0).astype(jnp.float32) * slot_weight[:, None]
    ).astype(jnp.bfloat16)
    send_inputs = send_inputs.reshape(expert_count, capacity, model_width)
    send_grads = send_grads.reshape(expert_count, capacity, model_width)
    up_local = up_weight[0]
    down_local = down_weight[0]
    arrived = (
        lax.all_to_all(send_inputs, "expert", split_axis=0, concat_axis=0, tiled=True),
        lax.all_to_all(send_grads, "expert", split_axis=0, concat_axis=0, tiled=True),
    )
    sender_count = arrived[0].shape[0]
    item_count = arrived[0].shape[1]
    result = expert_rows(
        arrived[0].reshape(sender_count * item_count, model_width),
        arrived[1].reshape(sender_count * item_count, model_width),
        up_local,
        down_local,
    )
    returned = lax.all_to_all(
        result.reshape(sender_count, item_count, model_width),
        "expert",
        split_axis=0,
        concat_axis=0,
        tiled=True,
    )
    residual_grad = combine_rows(grad_out, slot_place, returned)
    grad_rows = jnp.dot(
        lax.all_gather(residual_grad, "expert", axis=0, tiled=True),
        out_weight.T,
        preferred_element_type=jnp.float32,
    )
    out_grad = grad_rows.astype(jnp.bfloat16).reshape(
        block_count, SPAN, group_count, per_group, P_SIZE
    )
    grad_weighted, local_start = backward_terms(cumulative, out_grad, out_basis)
    device_grad, _ = chain_backward(block_decay, local_start, zero_state)

    def backward_turn(turn_index, incoming):
        return from_behind(
            (device_decay[..., None, None] * incoming + device_grad).astype(jnp.bfloat16), "seq", -1
        ).astype(jnp.float32)

    leave_grad = lax.fori_loop(0, lax.axis_size("seq") - 1, backward_turn, zero_state)
    _, leaving = chain_backward(block_decay, local_start, leave_grad)
    mixed_grad, in_grad, out_part = block_grads(
        cumulative,
        in_scale,
        mixed_act,
        out_grad,
        in_basis,
        out_basis,
        mixed_weighted,
        grad_weighted,
        entering,
        leaving,
        step_blocks,
        skip_heads,
    )
    value_grad = mixed_grad.reshape(seq_length, head_count * P_SIZE) * silu_grad(pre_value)
    after_rows = from_behind(value_grad[: KW - 1], "seq", -1)
    conv_grad = filter_back(value_grad, conv_weight, after_rows).astype(jnp.bfloat16)
    input_basis_grad = in_grad.reshape(seq_length, group_count * N).astype(jnp.bfloat16)
    output_basis_grad = out_part.reshape(seq_length, group_count * N).astype(jnp.bfloat16)
    return (residual_grad, conv_grad, input_basis_grad, output_basis_grad)


def solution(mesh):
    in_specs = (
        P(("seq", "expert"), None),
        P(("seq", "expert"), None),
        P(("seq", "expert"), None),
        P(("seq", "expert"), None),
        P("expert", None, None),
        P("expert", None, None),
        P("expert", None),
        P("seq", "expert"),
        P(None, "expert"),
        P("expert", "seq"),
        P("expert", "seq"),
        P("expert"),
        P("seq", "expert"),
        P("seq", "expert"),
    )
    out_specs = (
        P(("seq", "expert"), None),
        P("seq", "expert"),
        P("seq", "expert"),
        P("seq", "expert"),
    )
    return jax.shard_map(shards, mesh=mesh, in_specs=in_specs, out_specs=out_specs, check_vma=False)
```

profile of v0, /device:TPU:24, one launch (start us, length us, event | category | flops | bytes accessed | tf_op | source)
XLA Modules:
  0.0 1003.8 jit_solution(10444084823362101818)
XLA Ops:
  34.6 17.5 %all-to-all-done.1 = bf16[8,64,2048]{2,1,0:T(8,128)(2,1)} async-done(((bf16[8,64,2048]{2,1,0:T(8,128)(2,1)}), bf16[8,64,2048]{2,1,0:T(8,128)(2,1)}, u32[]{:S(2)}, u32[]{:S(2)}) %all-to-all-start.1) | async-done | bytes 2097184 | tf_op jit(solution)/shard_map/all_to_all | solution.py:224
  61.9 21.7 %all-to-all-done = bf16[8,64,2048]{2,1,0:T(8,128)(2,1)} async-done(((bf16[8,64,2048]{2,1,0:T(8,128)(2,1)}), bf16[8,64,2048]{2,1,0:T(8,128)(2,1)}, u32[]{:S(2)}, u32[]{:S(2)}) %all-to-all-start) | async-done | bytes 2097184 | tf_op jit(solution)/shard_map/all_to_all | solution.py:223
  83.6 7.3 fusion.12
  95.6 26.2 %all-to-all-done.2 = bf16[8,64,2048]{2,1,0:T(8,128)(2,1)S(1)} async-done(((bf16[8,64,2048]{2,1,0:T(8,128)(2,1)}), bf16[8,64,2048]{2,1,0:T(8,128)(2,1)S(1)}, u32[]{:S(2)}, u32[]{:S(2)}) %all-to-all-start.2) | async-done | bytes 2097184 | tf_op jit(solution)/shard_map/all_to_all | solution.py:234
  137.3 27.1 %all-gather.2.cloned.1.call-done = bf16[1024,2048]{1,0:T(8,128)(2,1)} async-done(((bf16[128,2048]{1,0:T(8,128)(2,1)}), bf16[1024,2048]{1,0:T(8,128)(2,1)}) %all-gather.2.cloned.1.call-update) | async-done | bytes 4194320 | tf_op jit(solution)/shard_map/all_gather | solution.py:243
  181.7 14.6 %while.78 = (s32[]{:T(128)}, f32[1,8,128,64]{3,2,1,0:T(8,128)S(1)}, f32[8,1,8]{2,1,0:T(1,128)}, f32[8,1,8,128,64]{4,3,2,1,0:T(8,128)}, s32[]{:T(128)}, /*index=5*/s32[]{:T(128)}, s32[]{:T(128)}) while((s32[]{:T(128)}, f32[1,8,128,64]{3,2,1,0:T(8,128)S(1)}, f32[8,1,8]{2,1,0:T(1,128)}, f32[8,1,8,128,64]{4,3,2,1,0:T(8,128)}, ...), condition=%wide.region_10.12_spmd.clone, body=%wide.region_9.11_spmd.clone.sunk | while | flops 196612 | bytes 786643 | solution.py:91
  196.3 351.1 %while.79 = (s32[]{:T(128)}, f32[1,8,128,64]{3,2,1,0:T(8,128)S(1)}, f32[1,8]{1,0:T(1,128)S(1)}, f32[1,8,128,64]{3,2,1,0:T(8,128)S(1)}, s32[]{:T(128)}, /*index=5*/s32[]{:T(128)}) while((s32[]{:T(128)}, f32[1,8,128,64]{3,2,1,0:T(8,128)S(1)}, f32[1,8]{1,0:T(1,128)S(1)}, f32[1,8,128,64]{3,2,1,0:T(8,128)S(1)}, s32[]{:T(128)}, ...), condition=%wide.region_12.14_spmd.clone, body=%wide.region_11.13_spmd.clone.sunk | while | flops 327683 | bytes 1573015 | solution.py:258
  208.1 6.5 collective-permute-start
  219.9 6.5 collective-permute-start
  230.8 6.5 collective-permute-start
  241.4 6.5 collective-permute-start
  252.0 6.5 collective-permute-start
  298.1 6.5 collective-permute-start
  549.2 20.8 %while.76 = (s32[]{:T(128)}, f32[1,8,128,64]{3,2,1,0:T(8,128)S(1)}, bf16[8,1,8,128,64]{4,3,2,1,0:T(8,128)(2,1)}, f32[8,1,8]{2,1,0:T(1,128)}, f32[8,1,8,128,64]{4,3,2,1,0:T(8,128)}, /*index=5*/s32[]{:T(128)}, s32[]{:T(128)}) while((s32[]{:T(128)}, f32[1,8,128,64]{3,2,1,0:T(8,128)S(1)}, bf16[8,1,8,128,64]{4,3,2,1,0:T(8,128)(2,1)}, ...), condition=%wide.region_14.16_spmd, body=%wide.region_13.15_spmd.sunk | while | flops 131075 | bytes 1573069 | solution.py:91
  598.0 14.6 %while.80 = (s32[]{:T(128)}, f32[1,8,128,64]{3,2,1,0:T(8,128)S(1)}, f32[8,1,8]{2,1,0:T(1,128)}, f32[8,1,8,128,64]{4,3,2,1,0:T(8,128)}, s32[]{:T(128)}, /*index=5*/s32[]{:T(128)}) while((s32[]{:T(128)}, f32[1,8,128,64]{3,2,1,0:T(8,128)S(1)}, f32[8,1,8]{2,1,0:T(1,128)}, f32[8,1,8,128,64]{4,3,2,1,0:T(8,128)}, s32[]{:T(128)}, ...), condition=%wide.region_17.19_spmd.clone, body=%wide.region_16.18_spmd.clone.sunk | while | flops 196611 | bytes 786623 | solution.py:85
  612.6 349.9 %while.81 = (s32[]{:T(128)}, f32[1,8,128,64]{3,2,1,0:T(8,128)S(1)}, f32[1,8]{1,0:T(1,128)S(1)}, f32[1,8,128,64]{3,2,1,0:T(8,128)S(1)}, s32[]{:T(128)}, /*index=5*/s32[]{:T(128)}) while((s32[]{:T(128)}, f32[1,8,128,64]{3,2,1,0:T(8,128)S(1)}, f32[1,8]{1,0:T(1,128)S(1)}, f32[1,8,128,64]{3,2,1,0:T(8,128)S(1)}, s32[]{:T(128)}, ...), condition=%wide.region_19.21_spmd.clone, body=%wide.region_18.20_spmd.clone.sunk | while | flops 327683 | bytes 1573015 | solution.py:205
  614.7 8.4 collective-permute-done.1
  625.2 8.4 collective-permute-done.1
  635.8 9.5 collective-permute-done.1
  647.4 10.7 %collective-permute-done.1 = bf16[1,8,128,64]{3,2,1,0:T(8,128)(2,1)S(1)} collective-permute-done((bf16[1,8,128,64]{3,2,1,0:T(8,128)(2,1)S(1)}, bf16[1,8,128,64]{3,2,1,0:T(8,128)(2,1)S(1)}, u32[]{:S(2)}, u32[]{:S(2)}) %collective-permute-start.1) | collective-permute-done | bytes 131104 | tf_op jit(solution)/shard_map/while/body/eval_jaxpr/ppermute | solution.py:15
  660.2 10.7 %collective-permute-done.1 = bf16[1,8,128,64]{3,2,1,0:T(8,128)(2,1)S(1)} collective-permute-done((bf16[1,8,128,64]{3,2,1,0:T(8,128)(2,1)S(1)}, bf16[1,8,128,64]{3,2,1,0:T(8,128)(2,1)S(1)}, u32[]{:S(2)}, u32[]{:S(2)}) %collective-permute-start.1) | collective-permute-done | bytes 131104 | tf_op jit(solution)/shard_map/while/body/eval_jaxpr/ppermute | solution.py:15
  673.0 9.9 collective-permute-done.1
  685.1 9.0 collective-permute-done.1
  696.2 8.4 collective-permute-done.1
  706.8 8.4 collective-permute-done.1
  717.3 8.4 collective-permute-done.1
  727.9 8.4 collective-permute-done.1
  738.5 9.5 collective-permute-done.1
  750.1 10.7 %collective-permute-done.1 = bf16[1,8,128,64]{3,2,1,0:T(8,128)(2,1)S(1)} collective-permute-done((bf16[1,8,128,64]{3,2,1,0:T(8,128)(2,1)S(1)}, bf16[1,8,128,64]{3,2,1,0:T(8,128)(2,1)S(1)}, u32[]{:S(2)}, u32[]{:S(2)}) %collective-permute-start.1) | collective-permute-done | bytes 131104 | tf_op jit(solution)/shard_map/while/body/eval_jaxpr/ppermute | solution.py:15
  762.9 10.6 %collective-permute-done.1 = bf16[1,8,128,64]{3,2,1,0:T(8,128)(2,1)S(1)} collective-permute-done((bf16[1,8,128,64]{3,2,1,0:T(8,128)(2,1)S(1)}, bf16[1,8,128,64]{3,2,1,0:T(8,128)(2,1)S(1)}, u32[]{:S(2)}, u32[]{:S(2)}) %collective-permute-start.1) | collective-permute-done | bytes 131104 | tf_op jit(solution)/shard_map/while/body/eval_jaxpr/ppermute | solution.py:15
  775.7 9.8 collective-permute-done.1
  787.7 8.9 collective-permute-done.1
  798.7 8.4 collective-permute-done.1
  809.3 8.4 collective-permute-done.1
  819.8 8.4 collective-permute-done.1
  830.4 8.5 collective-permute-done.1
  841.0 9.5 collective-permute-done.1
  852.7 10.8 %collective-permute-done.1 = bf16[1,8,128,64]{3,2,1,0:T(8,128)(2,1)S(1)} collective-permute-done((bf16[1,8,128,64]{3,2,1,0:T(8,128)(2,1)S(1)}, bf16[1,8,128,64]{3,2,1,0:T(8,128)(2,1)S(1)}, u32[]{:S(2)}, u32[]{:S(2)}) %collective-permute-start.1) | collective-permute-done | bytes 131104 | tf_op jit(solution)/shard_map/while/body/eval_jaxpr/ppermute | solution.py:15
  865.5 10.6 %collective-permute-done.1 = bf16[1,8,128,64]{3,2,1,0:T(8,128)(2,1)S(1)} collective-permute-done((bf16[1,8,128,64]{3,2,1,0:T(8,128)(2,1)S(1)}, bf16[1,8,128,64]{3,2,1,0:T(8,128)(2,1)S(1)}, u32[]{:S(2)}, u32[]{:S(2)}) %collective-permute-start.1) | collective-permute-done | bytes 131104 | tf_op jit(solution)/shard_map/while/body/eval_jaxpr/ppermute | solution.py:15
  878.3 9.8 collective-permute-done.1
  890.2 8.9 collective-permute-done.1
  901.2 8.4 collective-permute-done.1
  911.7 8.4 collective-permute-done.1
  922.3 8.4 collective-permute-done.1
  932.9 8.4 collective-permute-done.1
  943.4 8.4 collective-permute-done.1
  954.0 8.4 collective-permute-done.1
  964.3 20.7 %while.77 = (s32[]{:T(128)}, f32[1,8,128,64]{3,2,1,0:T(8,128)S(1)}, bf16[8,1,8,128,64]{4,3,2,1,0:T(8,128)(2,1)}, f32[8,1,8]{2,1,0:T(1,128)}, f32[8,1,8,128,64]{4,3,2,1,0:T(8,128)}, /*index=5*/s32[]{:T(128)}) while((s32[]{:T(128)}, f32[1,8,128,64]{3,2,1,0:T(8,128)S(1)}, bf16[8,1,8,128,64]{4,3,2,1,0:T(8,128)(2,1)}, f32[8,1,8]{2,1,0:T(1,128)}, ...), condition=%wide.region_21.23_spmd, body=%wide.region_20.22_spmd.sunk | while | flops 131074 | bytes 1573049 | solution.py:85
  (432 shorter events, 563.7 us)
Async XLA Ops:
  20.5 31.6 %all-to-all-start.1 = ((bf16[8,64,2048]{2,1,0:T(8,128)(2,1)}), bf16[8,64,2048]{2,1,0:T(8,128)(2,1)}, u32[]{:S(2)}, u32[]{:S(2)}) async-start(bf16[8,64,2048]{2,1,0:T(8,128)(2,1)} %bitcast.209), calls=%async_computation.1 | async-start | bytes 4194304 | tf_op jit(solution)/shard_map/all_to_all | solution.py:224
  52.1 31.5 %all-to-all-start = ((bf16[8,64,2048]{2,1,0:T(8,128)(2,1)}), bf16[8,64,2048]{2,1,0:T(8,128)(2,1)}, u32[]{:S(2)}, u32[]{:S(2)}) async-start(bf16[8,64,2048]{2,1,0:T(8,128)(2,1)} %bitcast.208), calls=%async_computation | async-start | bytes 4194304 | tf_op jit(solution)/shard_map/all_to_all | solution.py:223
  90.9 30.9 %all-to-all-start.2 = ((bf16[8,64,2048]{2,1,0:T(8,128)(2,1)}), bf16[8,64,2048]{2,1,0:T(8,128)(2,1)S(1)}, u32[]{:S(2)}, u32[]{:S(2)}) async-start(bf16[8,64,2048]{2,1,0:T(8,128)(2,1)} %bitcast.223), calls=%async_computation.2 | async-start | bytes 4194304 | tf_op jit(solution)/shard_map/all_to_all | solution.py:234
  94.7 69.7 %all-gather.2.cloned.1.call-start = ((), (), s32[]{:S(2)}) async-start(), calls=%async_computation.3 | async-start | bytes 4718592 | tf_op jit(solution)/shard_map/all_gather | solution.py:243
  196.4 11.5 %collective-permute-start = (bf16[1,8,128,64]{3,2,1,0:T(8,128)(2,1)S(1)}, bf16[1,8,128,64]{3,2,1,0:T(8,128)(2,1)S(1)}, u32[]{:S(2)}, u32[]{:S(2)}) collective-permute-start(bf16[1,8,128,64]{3,2,1,0:T(8,128)(2,1)S(1)} %fusion.99), channel_id=1, source_target_pairs={{8,0},{16,8},{24,16},{32,24},{40,32},{48,40},{56,48},{64,56},{72,6... | collective-permute-start | bytes 393224 | tf_op jit(solution)/shard_map/while/body/eval_jaxpr/ppermute | solution.py:15
  208.1 11.7 %collective-permute-start = (bf16[1,8,128,64]{3,2,1,0:T(8,128)(2,1)S(1)}, bf16[1,8,128,64]{3,2,1,0:T(8,128)(2,1)S(1)}, u32[]{:S(2)}, u32[]{:S(2)}) collective-permute-start(bf16[1,8,128,64]{3,2,1,0:T(8,128)(2,1)S(1)} %fusion.99), channel_id=1, source_target_pairs={{8,0},{16,8},{24,16},{32,24},{40,32},{48,40},{56,48},{64,56},{72,6... | collective-permute-start | bytes 393224 | tf_op jit(solution)/shard_map/while/body/eval_jaxpr/ppermute | solution.py:15
  219.9 10.7 %collective-permute-start = (bf16[1,8,128,64]{3,2,1,0:T(8,128)(2,1)S(1)}, bf16[1,8,128,64]{3,2,1,0:T(8,128)(2,1)S(1)}, u32[]{:S(2)}, u32[]{:S(2)}) collective-permute-start(bf16[1,8,128,64]{3,2,1,0:T(8,128)(2,1)S(1)} %fusion.99), channel_id=1, source_target_pairs={{8,0},{16,8},{24,16},{32,24},{40,32},{48,40},{56,48},{64,56},{72,6... | collective-permute-start | bytes 393224 | tf_op jit(solution)/shard_map/while/body/eval_jaxpr/ppermute | solution.py:15
  230.8 10.4 %collective-permute-start = (bf16[1,8,128,64]{3,2,1,0:T(8,128)(2,1)S(1)}, bf16[1,8,128,64]{3,2,1,0:T(8,128)(2,1)S(1)}, u32[]{:S(2)}, u32[]{:S(2)}) collective-permute-start(bf16[1,8,128,64]{3,2,1,0:T(8,128)(2,1)S(1)} %fusion.99), channel_id=1, source_target_pairs={{8,0},{16,8},{24,16},{32,24},{40,32},{48,40},{56,48},{64,56},{72,6... | collective-permute-start | bytes 393224 | tf_op jit(solution)/shard_map/while/body/eval_jaxpr/ppermute | solution.py:15
  241.4 10.4 %collective-permute-start = (bf16[1,8,128,64]{3,2,1,0:T(8,128)(2,1)S(1)}, bf16[1,8,128,64]{3,2,1,0:T(8,128)(2,1)S(1)}, u32[]{:S(2)}, u32[]{:S(2)}) collective-permute-start(bf16[1,8,128,64]{3,2,1,0:T(8,128)(2,1)S(1)} %fusion.99), channel_id=1, source_target_pairs={{8,0},{16,8},{24,16},{32,24},{40,32},{48,40},{56,48},{64,56},{72,6... | collective-permute-start | bytes 393224 | tf_op jit(solution)/shard_map/while/body/eval_jaxpr/ppermute | solution.py:15
  262.5 10.5 %collective-permute-start = (bf16[1,8,128,64]{3,2,1,0:T(8,128)(2,1)S(1)}, bf16[1,8,128,64]{3,2,1,0:T(8,128)(2,1)S(1)}, u32[]{:S(2)}, u32[]{:S(2)}) collective-permute-start(bf16[1,8,128,64]{3,2,1,0:T(8,128)(2,1)S(1)} %fusion.99), channel_id=1, source_target_pairs={{8,0},{16,8},{24,16},{32,24},{40,32},{48,40},{56,48},{64,56},{72,6... | collective-permute-start | bytes 393224 | tf_op jit(solution)/shard_map/while/body/eval_jaxpr/ppermute | solution.py:15
  273.3 11.6 %collective-permute-start = (bf16[1,8,128,64]{3,2,1,0:T(8,128)(2,1)S(1)}, bf16[1,8,128,64]{3,2,1,0:T(8,128)(2,1)S(1)}, u32[]{:S(2)}, u32[]{:S(2)}) collective-permute-start(bf16[1,8,128,64]{3,2,1,0:T(8,128)(2,1)S(1)} %fusion.99), channel_id=1, source_target_pairs={{8,0},{16,8},{24,16},{32,24},{40,32},{48,40},{56,48},{64,56},{72,6... | collective-permute-start | bytes 393224 | tf_op jit(solution)/shard_map/while/body/eval_jaxpr/ppermute | solution.py:15
  285.1 12.8 %collective-permute-start = (bf16[1,8,128,64]{3,2,1,0:T(8,128)(2,1)S(1)}, bf16[1,8,128,64]{3,2,1,0:T(8,128)(2,1)S(1)}, u32[]{:S(2)}, u32[]{:S(2)}) collective-permute-start(bf16[1,8,128,64]{3,2,1,0:T(8,128)(2,1)S(1)} %fusion.99), channel_id=1, source_target_pairs={{8,0},{16,8},{24,16},{32,24},{40,32},{48,40},{56,48},{64,56},{72,6... | collective-permute-start | bytes 393224 | tf_op jit(solution)/shard_map/while/body/eval_jaxpr/ppermute | solution.py:15
  298.1 12.4 %collective-permute-start = (bf16[1,8,128,64]{3,2,1,0:T(8,128)(2,1)S(1)}, bf16[1,8,128,64]{3,2,1,0:T(8,128)(2,1)S(1)}, u32[]{:S(2)}, u32[]{:S(2)}) collective-permute-start(bf16[1,8,128,64]{3,2,1,0:T(8,128)(2,1)S(1)} %fusion.99), channel_id=1, source_target_pairs={{8,0},{16,8},{24,16},{32,24},{40,32},{48,40},{56,48},{64,56},{72,6... | collective-permute-start | bytes 393224 | tf_op jit(solution)/shard_map/while/body/eval_jaxpr/ppermute | solution.py:15
  310.7 11.6 %collective-permute-start = (bf16[1,8,128,64]{3,2,1,0:T(8,128)(2,1)S(1)}, bf16[1,8,128,64]{3,2,1,0:T(8,128)(2,1)S(1)}, u32[]{:S(2)}, u32[]{:S(2)}) collective-permute-start(bf16[1,8,128,64]{3,2,1,0:T(8,128)(2,1)S(1)} %fusion.99), channel_id=1, source_target_pairs={{8,0},{16,8},{24,16},{32,24},{40,32},{48,40},{56,48},{64,56},{72,6... | collective-permute-start | bytes 393224 | tf_op jit(solution)/shard_map/while/body/eval_jaxpr/ppermute | solution.py:15
  322.4 10.6 %collective-permute-start = (bf16[1,8,128,64]{3,2,1,0:T(8,128)(2,1)S(1)}, bf16[1,8,128,64]{3,2,1,0:T(8,128)(2,1)S(1)}, u32[]{:S(2)}, u32[]{:S(2)}) collective-permute-start(bf16[1,8,128,64]{3,2,1,0:T(8,128)(2,1)S(1)} %fusion.99), channel_id=1, source_target_pairs={{8,0},{16,8},{24,16},{32,24},{40,32},{48,40},{56,48},{64,56},{72,6... | collective-permute-start | bytes 393224 | tf_op jit(solution)/shard_map/while/body/eval_jaxpr/ppermute | solution.py:15
  343.8 10.4 %collective-permute-start = (bf16[1,8,128,64]{3,2,1,0:T(8,128)(2,1)S(1)}, bf16[1,8,128,64]{3,2,1,0:T(8,128)(2,1)S(1)}, u32[]{:S(2)}, u32[]{:S(2)}) collective-permute-start(bf16[1,8,128,64]{3,2,1,0:T(8,128)(2,1)S(1)} %fusion.99), channel_id=1, source_target_pairs={{8,0},{16,8},{24,16},{32,24},{40,32},{48,40},{56,48},{64,56},{72,6... | collective-permute-start | bytes 393224 | tf_op jit(solution)/shard_map/while/body/eval_jaxpr/ppermute | solution.py:15
  354.4 10.4 %collective-permute-start = (bf16[1,8,128,64]{3,2,1,0:T(8,128)(2,1)S(1)}, bf16[1,8,128,64]{3,2,1,0:T(8,128)(2,1)S(1)}, u32[]{:S(2)}, u32[]{:S(2)}) collective-permute-start(bf16[1,8,128,64]{3,2,1,0:T(8,128)(2,1)S(1)} %fusion.99), channel_id=1, source_target_pairs={{8,0},{16,8},{24,16},{32,24},{40,32},{48,40},{56,48},{64,56},{72,6... | collective-permute-start | bytes 393224 | tf_op jit(solution)/shard_map/while/body/eval_jaxpr/ppermute | solution.py:15
  364.9 10.6 %collective-permute-start = (bf16[1,8,128,64]{3,2,1,0:T(8,128)(2,1)S(1)}, bf16[1,8,128,64]{3,2,1,0:T(8,128)(2,1)S(1)}, u32[]{:S(2)}, u32[]{:S(2)}) collective-permute-start(bf16[1,8,128,64]{3,2,1,0:T(8,128)(2,1)S(1)} %fusion.99), channel_id=1, source_target_pairs={{8,0},{16,8},{24,16},{32,24},{40,32},{48,40},{56,48},{64,56},{72,6... | collective-permute-start | bytes 393224 | tf_op jit(solution)/shard_map/while/body/eval_jaxpr/ppermute | solution.py:15
  375.7 11.7 %collective-permute-start = (bf16[1,8,128,64]{3,2,1,0:T(8,128)(2,1)S(1)}, bf16[1,8,128,64]{3,2,1,0:T(8,128)(2,1)S(1)}, u32[]{:S(2)}, u32[]{:S(2)}) collective-permute-start(bf16[1,8,128,64]{3,2,1,0:T(8,128)(2,1)S(1)} %fusion.99), channel_id=1, source_target_pairs={{8,0},{16,8},{24,16},{32,24},{40,32},{48,40},{56,48},{64,56},{72,6... | collective-permute-start | bytes 393224 | tf_op jit(solution)/shard_map/while/body/eval_jaxpr/ppermute | solution.py:15
  387.6 12.8 %collective-permute-start = (bf16[1,8,128,64]{3,2,1,0:T(8,128)(2,1)S(1)}, bf16[1,8,128,64]{3,2,1,0:T(8,128)(2,1)S(1)}, u32[]{:S(2)}, u32[]{:S(2)}) collective-permute-start(bf16[1,8,128,64]{3,2,1,0:T(8,128)(2,1)S(1)} %fusion.99), channel_id=1, source_target_pairs={{8,0},{16,8},{24,16},{32,24},{40,32},{48,40},{56,48},{64,56},{72,6... | collective-permute-start | bytes 393224 | tf_op jit(solution)/shard_map/while/body/eval_jaxpr/ppermute | solution.py:15
  400.7 12.4 %collective-permute-start = (bf16[1,8,128,64]{3,2,1,0:T(8,128)(2,1)S(1)}, bf16[1,8,128,64]{3,2,1,0:T(8,128)(2,1)S(1)}, u32[]{:S(2)}, u32[]{:S(2)}) collective-permute-start(bf16[1,8,128,64]{3,2,1,0:T(8,128)(2,1)S(1)} %fusion.99), channel_id=1, source_target_pairs={{8,0},{16,8},{24,16},{32,24},{40,32},{48,40},{56,48},{64,56},{72,6... | collective-permute-start | bytes 393224 | tf_op jit(solution)/shard_map/while/body/eval_jaxpr/ppermute | solution.py:15
  413.2 11.5 %collective-permute-start = (bf16[1,8,128,64]{3,2,1,0:T(8,128)(2,1)S(1)}, bf16[1,8,128,64]{3,2,1,0:T(8,128)(2,1)S(1)}, u32[]{:S(2)}, u32[]{:S(2)}) collective-permute-start(bf16[1,8,128,64]{3,2,1,0:T(8,128)(2,1)S(1)} %fusion.99), channel_id=1, source_target_pairs={{8,0},{16,8},{24,16},{32,24},{40,32},{48,40},{56,48},{64,56},{72,6... | collective-permute-start | bytes 393224 | tf_op jit(solution)/shard_map/while/body/eval_jaxpr/ppermute | solution.py:15
  425.0 10.6 %collective-permute-start = (bf16[1,8,128,64]{3,2,1,0:T(8,128)(2,1)S(1)}, bf16[1,8,128,64]{3,2,1,0:T(8,128)(2,1)S(1)}, u32[]{:S(2)}, u32[]{:S(2)}) collective-permute-start(bf16[1,8,128,64]{3,2,1,0:T(8,128)(2,1)S(1)} %fusion.99), channel_id=1, source_target_pairs={{8,0},{16,8},{24,16},{32,24},{40,32},{48,40},{56,48},{64,56},{72,6... | collective-permute-start | bytes 393224 | tf_op jit(solution)/shard_map/while/body/eval_jaxpr/ppermute | solution.py:15
  435.8 10.4 %collective-permute-start = (bf16[1,8,128,64]{3,2,1,0:T(8,128)(2,1)S(1)}, bf16[1,8,128,64]{3,2,1,0:T(8,128)(2,1)S(1)}, u32[]{:S(2)}, u32[]{:S(2)}) collective-permute-start(bf16[1,8,128,64]{3,2,1,0:T(8,128)(2,1)S(1)} %fusion.99), channel_id=1, source_target_pairs={{8,0},{16,8},{24,16},{32,24},{40,32},{48,40},{56,48},{64,56},{72,6... | collective-permute-start | bytes 393224 | tf_op jit(solution)/shard_map/while/body/eval_jaxpr/ppermute | solution.py:15
  446.3 10.4 %collective-permute-start = (bf16[1,8,128,64]{3,2,1,0:T(8,128)(2,1)S(1)}, bf16[1,8,128,64]{3,2,1,0:T(8,128)(2,1)S(1)}, u32[]{:S(2)}, u32[]{:S(2)}) collective-permute-start(bf16[1,8,128,64]{3,2,1,0:T(8,128)(2,1)S(1)} %fusion.99), channel_id=1, source_target_pairs={{8,0},{16,8},{24,16},{32,24},{40,32},{48,40},{56,48},{64,56},{72,6... | collective-permute-start | bytes 393224 | tf_op jit(solution)/shard_map/while/body/eval_jaxpr/ppermute | solution.py:15
  467.5 10.6 %collective-permute-start = (bf16[1,8,128,64]{3,2,1,0:T(8,128)(2,1)S(1)}, bf16[1,8,128,64]{3,2,1,0:T(8,128)(2,1)S(1)}, u32[]{:S(2)}, u32[]{:S(2)}) collective-permute-start(bf16[1,8,128,64]{3,2,1,0:T(8,128)(2,1)S(1)} %fusion.99), channel_id=1, source_target_pairs={{8,0},{16,8},{24,16},{32,24},{40,32},{48,40},{56,48},{64,56},{72,6... | collective-permute-start | bytes 393224 | tf_op jit(solution)/shard_map/while/body/eval_jaxpr/ppermute | solution.py:15
  478.3 11.7 %collective-permute-start = (bf16[1,8,128,64]{3,2,1,0:T(8,128)(2,1)S(1)}, bf16[1,8,128,64]{3,2,1,0:T(8,128)(2,1)S(1)}, u32[]{:S(2)}, u32[]{:S(2)}) collective-permute-start(bf16[1,8,128,64]{3,2,1,0:T(8,128)(2,1)S(1)} %fusion.99), channel_id=1, source_target_pairs={{8,0},{16,8},{24,16},{32,24},{40,32},{48,40},{56,48},{64,56},{72,6... | collective-permute-start | bytes 393224 | tf_op jit(solution)/shard_map/while/body/eval_jaxpr/ppermute | solution.py:15
  490.2 12.9 %collective-permute-start = (bf16[1,8,128,64]{3,2,1,0:T(8,128)(2,1)S(1)}, bf16[1,8,128,64]{3,2,1,0:T(8,128)(2,1)S(1)}, u32[]{:S(2)}, u32[]{:S(2)}) collective-permute-start(bf16[1,8,128,64]{3,2,1,0:T(8,128)(2,1)S(1)} %fusion.99), channel_id=1, source_target_pairs={{8,0},{16,8},{24,16},{32,24},{40,32},{48,40},{56,48},{64,56},{72,6... | collective-permute-start | bytes 393224 | tf_op jit(solution)/shard_map/while/body/eval_jaxpr/ppermute | solution.py:15
  503.3 12.3 %collective-permute-start = (bf16[1,8,128,64]{3,2,1,0:T(8,128)(2,1)S(1)}, bf16[1,8,128,64]{3,2,1,0:T(8,128)(2,1)S(1)}, u32[]{:S(2)}, u32[]{:S(2)}) collective-permute-start(bf16[1,8,128,64]{3,2,1,0:T(8,128)(2,1)S(1)} %fusion.99), channel_id=1, source_target_pairs={{8,0},{16,8},{24,16},{32,24},{40,32},{48,40},{56,48},{64,56},{72,6... | collective-permute-start | bytes 393224 | tf_op jit(solution)/shard_map/while/body/eval_jaxpr/ppermute | solution.py:15
  515.8 10.4 %collective-permute-start = (bf16[1,8,128,64]{3,2,1,0:T(8,128)(2,1)S(1)}, bf16[1,8,128,64]{3,2,1,0:T(8,128)(2,1)S(1)}, u32[]{:S(2)}, u32[]{:S(2)}) collective-permute-start(bf16[1,8,128,64]{3,2,1,0:T(8,128)(2,1)S(1)} %fusion.99), channel_id=1, source_target_pairs={{8,0},{16,8},{24,16},{32,24},{40,32},{48,40},{56,48},{64,56},{72,6... | collective-permute-start | bytes 393224 | tf_op jit(solution)/shard_map/while/body/eval_jaxpr/ppermute | solution.py:15
  526.4 10.4 %collective-permute-start = (bf16[1,8,128,64]{3,2,1,0:T(8,128)(2,1)S(1)}, bf16[1,8,128,64]{3,2,1,0:T(8,128)(2,1)S(1)}, u32[]{:S(2)}, u32[]{:S(2)}) collective-permute-start(bf16[1,8,128,64]{3,2,1,0:T(8,128)(2,1)S(1)} %fusion.99), channel_id=1, source_target_pairs={{8,0},{16,8},{24,16},{32,24},{40,32},{48,40},{56,48},{64,56},{72,6... | collective-permute-start | bytes 393224 | tf_op jit(solution)/shard_map/while/body/eval_jaxpr/ppermute | solution.py:15
  587.7 401.9 %collective-permute-start.2 = (f32[3,512]{0,1:T(8,128)}, f32[3,512]{0,1:T(8,128)}, u32[]{:S(2)}, u32[]{:S(2)}) collective-permute-start(f32[3,512]{0,1:T(8,128)} %slice.54), channel_id=1, source_target_pairs={{8,0},{16,8},{24,16},{32,24},{40,32},{48,40},{56,48},{64,56},{72,6... | collective-permute-start | bytes 18440 | tf_op jit(solution)/shard_map/ppermute | solution.py:15
  633.9 11.4 %collective-permute-start.1 = (bf16[1,8,128,64]{3,2,1,0:T(8,128)(2,1)S(1)}, bf16[1,8,128,64]{3,2,1,0:T(8,128)(2,1)S(1)}, u32[]{:S(2)}, u32[]{:S(2)}) collective-permute-start(bf16[1,8,128,64]{3,2,1,0:T(8,128)(2,1)S(1)} %fusion.100), channel_id=1, source_target_pairs={{0,8},{8,16},{16,24},{24,32},{32,40},{40,48},{48,56},{56,64},{64,7... | collective-permute-start | bytes 393224 | tf_op jit(solution)/shard_map/while/body/eval_jaxpr/ppermute | solution.py:15
  645.5 12.6 %collective-permute-start.1 = (bf16[1,8,128,64]{3,2,1,0:T(8,128)(2,1)S(1)}, bf16[1,8,128,64]{3,2,1,0:T(8,128)(2,1)S(1)}, u32[]{:S(2)}, u32[]{:S(2)}) collective-permute-start(bf16[1,8,128,64]{3,2,1,0:T(8,128)(2,1)S(1)} %fusion.100), channel_id=1, source_target_pairs={{0,8},{8,16},{16,24},{24,32},{32,40},{40,48},{48,56},{56,64},{64,7... | collective-permute-start | bytes 393224 | tf_op jit(solution)/shard_map/while/body/eval_jaxpr/ppermute | solution.py:15
  658.2 12.6 %collective-permute-start.1 = (bf16[1,8,128,64]{3,2,1,0:T(8,128)(2,1)S(1)}, bf16[1,8,128,64]{3,2,1,0:T(8,128)(2,1)S(1)}, u32[]{:S(2)}, u32[]{:S(2)}) collective-permute-start(bf16[1,8,128,64]{3,2,1,0:T(8,128)(2,1)S(1)} %fusion.100), channel_id=1, source_target_pairs={{0,8},{8,16},{16,24},{24,32},{32,40},{40,48},{48,56},{56,64},{64,7... | collective-permute-start | bytes 393224 | tf_op jit(solution)/shard_map/while/body/eval_jaxpr/ppermute | solution.py:15
  671.1 11.9 %collective-permute-start.1 = (bf16[1,8,128,64]{3,2,1,0:T(8,128)(2,1)S(1)}, bf16[1,8,128,64]{3,2,1,0:T(8,128)(2,1)S(1)}, u32[]{:S(2)}, u32[]{:S(2)}) collective-permute-start(bf16[1,8,128,64]{3,2,1,0:T(8,128)(2,1)S(1)} %fusion.100), channel_id=1, source_target_pairs={{0,8},{8,16},{16,24},{24,32},{32,40},{40,48},{48,56},{56,64},{64,7... | collective-permute-start | bytes 393224 | tf_op jit(solution)/shard_map/while/body/eval_jaxpr/ppermute | solution.py:15
  683.1 11.0 %collective-permute-start.1 = (bf16[1,8,128,64]{3,2,1,0:T(8,128)(2,1)S(1)}, bf16[1,8,128,64]{3,2,1,0:T(8,128)(2,1)S(1)}, u32[]{:S(2)}, u32[]{:S(2)}) collective-permute-start(bf16[1,8,128,64]{3,2,1,0:T(8,128)(2,1)S(1)} %fusion.100), channel_id=1, source_target_pairs={{0,8},{8,16},{16,24},{24,32},{32,40},{40,48},{48,56},{56,64},{64,7... | collective-permute-start | bytes 393224 | tf_op jit(solution)/shard_map/while/body/eval_jaxpr/ppermute | solution.py:15
  736.5 11.4 %collective-permute-start.1 = (bf16[1,8,128,64]{3,2,1,0:T(8,128)(2,1)S(1)}, bf16[1,8,128,64]{3,2,1,0:T(8,128)(2,1)S(1)}, u32[]{:S(2)}, u32[]{:S(2)}) collective-permute-start(bf16[1,8,128,64]{3,2,1,0:T(8,128)(2,1)S(1)} %fusion.100), channel_id=1, source_target_pairs={{0,8},{8,16},{16,24},{24,32},{32,40},{40,48},{48,56},{56,64},{64,7... | collective-permute-start | bytes 393224 | tf_op jit(solution)/shard_map/while/body/eval_jaxpr/ppermute | solution.py:15
  748.2 12.7 %collective-permute-start.1 = (bf16[1,8,128,64]{3,2,1,0:T(8,128)(2,1)S(1)}, bf16[1,8,128,64]{3,2,1,0:T(8,128)(2,1)S(1)}, u32[]{:S(2)}, u32[]{:S(2)}) collective-permute-start(bf16[1,8,128,64]{3,2,1,0:T(8,128)(2,1)S(1)} %fusion.100), channel_id=1, source_target_pairs={{0,8},{8,16},{16,24},{24,32},{32,40},{40,48},{48,56},{56,64},{64,7... | collective-permute-start | bytes 393224 | tf_op jit(solution)/shard_map/while/body/eval_jaxpr/ppermute | solution.py:15
  761.0 12.6 %collective-permute-start.1 = (bf16[1,8,128,64]{3,2,1,0:T(8,128)(2,1)S(1)}, bf16[1,8,128,64]{3,2,1,0:T(8,128)(2,1)S(1)}, u32[]{:S(2)}, u32[]{:S(2)}) collective-permute-start(bf16[1,8,128,64]{3,2,1,0:T(8,128)(2,1)S(1)} %fusion.100), channel_id=1, source_target_pairs={{0,8},{8,16},{16,24},{24,32},{32,40},{40,48},{48,56},{56,64},{64,7... | collective-permute-start | bytes 393224 | tf_op jit(solution)/shard_map/while/body/eval_jaxpr/ppermute | solution.py:15
  773.8 11.8 %collective-permute-start.1 = (bf16[1,8,128,64]{3,2,1,0:T(8,128)(2,1)S(1)}, bf16[1,8,128,64]{3,2,1,0:T(8,128)(2,1)S(1)}, u32[]{:S(2)}, u32[]{:S(2)}) collective-permute-start(bf16[1,8,128,64]{3,2,1,0:T(8,128)(2,1)S(1)} %fusion.100), channel_id=1, source_target_pairs={{0,8},{8,16},{16,24},{24,32},{32,40},{40,48},{48,56},{56,64},{64,7... | collective-permute-start | bytes 393224 | tf_op jit(solution)/shard_map/while/body/eval_jaxpr/ppermute | solution.py:15
  785.7 10.9 %collective-permute-start.1 = (bf16[1,8,128,64]{3,2,1,0:T(8,128)(2,1)S(1)}, bf16[1,8,128,64]{3,2,1,0:T(8,128)(2,1)S(1)}, u32[]{:S(2)}, u32[]{:S(2)}) collective-permute-start(bf16[1,8,128,64]{3,2,1,0:T(8,128)(2,1)S(1)} %fusion.100), channel_id=1, source_target_pairs={{0,8},{8,16},{16,24},{24,32},{32,40},{40,48},{48,56},{56,64},{64,7... | collective-permute-start | bytes 393224 | tf_op jit(solution)/shard_map/while/body/eval_jaxpr/ppermute | solution.py:15
  828.5 10.4 %collective-permute-start.1 = (bf16[1,8,128,64]{3,2,1,0:T(8,128)(2,1)S(1)}, bf16[1,8,128,64]{3,2,1,0:T(8,128)(2,1)S(1)}, u32[]{:S(2)}, u32[]{:S(2)}) collective-permute-start(bf16[1,8,128,64]{3,2,1,0:T(8,128)(2,1)S(1)} %fusion.100), channel_id=1, source_target_pairs={{0,8},{8,16},{16,24},{24,32},{32,40},{40,48},{48,56},{56,64},{64,7... | collective-permute-start | bytes 393224 | tf_op jit(solution)/shard_map/while/body/eval_jaxpr/ppermute | solution.py:15
  839.1 11.5 %collective-permute-start.1 = (bf16[1,8,128,64]{3,2,1,0:T(8,128)(2,1)S(1)}, bf16[1,8,128,64]{3,2,1,0:T(8,128)(2,1)S(1)}, u32[]{:S(2)}, u32[]{:S(2)}) collective-permute-start(bf16[1,8,128,64]{3,2,1,0:T(8,128)(2,1)S(1)} %fusion.100), channel_id=1, source_target_pairs={{0,8},{8,16},{16,24},{24,32},{32,40},{40,48},{48,56},{56,64},{64,7... | collective-permute-start | bytes 393224 | tf_op jit(solution)/shard_map/while/body/eval_jaxpr/ppermute | solution.py:15
  850.7 12.7 %collective-permute-start.1 = (bf16[1,8,128,64]{3,2,1,0:T(8,128)(2,1)S(1)}, bf16[1,8,128,64]{3,2,1,0:T(8,128)(2,1)S(1)}, u32[]{:S(2)}, u32[]{:S(2)}) collective-permute-start(bf16[1,8,128,64]{3,2,1,0:T(8,128)(2,1)S(1)} %fusion.100), channel_id=1, source_target_pairs={{0,8},{8,16},{16,24},{24,32},{32,40},{40,48},{48,56},{56,64},{64,7... | collective-permute-start | bytes 393224 | tf_op jit(solution)/shard_map/while/body/eval_jaxpr/ppermute | solution.py:15
  863.6 12.5 %collective-permute-start.1 = (bf16[1,8,128,64]{3,2,1,0:T(8,128)(2,1)S(1)}, bf16[1,8,128,64]{3,2,1,0:T(8,128)(2,1)S(1)}, u32[]{:S(2)}, u32[]{:S(2)}) collective-permute-start(bf16[1,8,128,64]{3,2,1,0:T(8,128)(2,1)S(1)} %fusion.100), channel_id=1, source_target_pairs={{0,8},{8,16},{16,24},{24,32},{32,40},{40,48},{48,56},{56,64},{64,7... | collective-permute-start | bytes 393224 | tf_op jit(solution)/shard_map/while/body/eval_jaxpr/ppermute | solution.py:15
  876.3 11.7 %collective-permute-start.1 = (bf16[1,8,128,64]{3,2,1,0:T(8,128)(2,1)S(1)}, bf16[1,8,128,64]{3,2,1,0:T(8,128)(2,1)S(1)}, u32[]{:S(2)}, u32[]{:S(2)}) collective-permute-start(bf16[1,8,128,64]{3,2,1,0:T(8,128)(2,1)S(1)} %fusion.100), channel_id=1, source_target_pairs={{0,8},{8,16},{16,24},{24,32},{32,40},{40,48},{48,56},{56,64},{64,7... | collective-permute-start | bytes 393224 | tf_op jit(solution)/shard_map/while/body/eval_jaxpr/ppermute | solution.py:15
  888.2 10.8 %collective-permute-start.1 = (bf16[1,8,128,64]{3,2,1,0:T(8,128)(2,1)S(1)}, bf16[1,8,128,64]{3,2,1,0:T(8,128)(2,1)S(1)}, u32[]{:S(2)}, u32[]{:S(2)}) collective-permute-start(bf16[1,8,128,64]{3,2,1,0:T(8,128)(2,1)S(1)} %fusion.100), channel_id=1, source_target_pairs={{0,8},{8,16},{16,24},{24,32},{32,40},{40,48},{48,56},{56,64},{64,7... | collective-permute-start | bytes 393224 | tf_op jit(solution)/shard_map/while/body/eval_jaxpr/ppermute | solution.py:15
  (47 other events, 391.7 us)
Sparse Core Ops, SparseCore 0:
  128.9 35.4 all-gather.1
where the time goes:
time: 1010 us; the launch traced here: 1000 us
  waiting for transfers between devices  521 us (52%)
  starting transfers between devices  279 us (28%)
  local copies, waits for them, and re-layouts  82 us (8%)
  other arithmetic  70.2 us (7%)
  matrix products  34.2 us (3%)
  between operations  14.6 us (1%)
    ppermute x63, waiting for transfers between devices, from_behind(): return lax.ppermute(value, axis, pairs)  429 us
    ppermute x63, starting transfers between devices, from_behind(): return lax.ppermute(value, axis, pairs)  266 us
    add x32, other arithmetic, advance(): return (pair_now[0][..., None, None] * state_now + pair_now[1], state_now)  37.4 us
    all_gather x1, waiting for transfers between devices, shards(): lax.all_gather(residual_grad, 'expert', axis=0, tiled=True)  27.1 us
    all_to_all x1, waiting for transfers between devices, shards(): lax.all_to_all(result.reshape(sender_count, item_count, model_width), 'ex...  26.2 us
    all_to_all x1, waiting for transfers between devices, shards(): lax.all_to_all(send_inputs, 'expert', split_axis=0, concat_axis=0, tiled=...  21.7 us
    mul x32, local copies, waits for them, and re-layouts, advance(): return (pair_now[0][..., None, None] * state_now + pair_now[1], state_now)  20.7 us
  transfers between devices with their start and end apart: 67, of which 66 were waited for; matrix products, arithmetic and copies ran while one was open for 7% of the time, Pallas kernels for 0%

commit v1 on v0

--- a/solution.py
+++ b/solution.py
@@ -7,6 +7,11 @@
 N = 128
 KW = 4
 SPAN = 128
+
+
+def tiled_gather(array, axis, dim):
+    copies = jnp.concatenate([array] * lax.axis_size(axis), axis=dim)
+    return lax.all_to_all(copies, axis, dim, dim, tiled=True)
 
 
 def from_behind(value, axis, by):
@@ -240,9 +245,7 @@
     )
     residual_grad = combine_rows(grad_out, slot_place, returned)
     grad_rows = jnp.dot(
-        lax.all_gather(residual_grad, "expert", axis=0, tiled=True),
-        out_weight.T,
-        preferred_element_type=jnp.float32,
+        tiled_gather(residual_grad, "expert", 0), out_weight.T, preferred_element_type=jnp.float32
     )
     out_grad = grad_rows.astype(jnp.bfloat16).reshape(
         block_count, SPAN, group_count, per_group, P_SIZE

time: 1010 us -> 1020 us (level)
  waiting for transfers between devices: 521 us -> 535 us
  between operations: 14.6 us -> 1.28 us
    all_to_all x0 -> x1, waiting for transfers between devices: none -> 41 us  [tiled_gather(): return lax.all_to_all(copies, axis, dim, dim, tiled=True)]
    all_gather x1 -> x0, waiting for transfers between devices: 27.1 us -> none  [shards(): lax.all_gather(residual_grad, 'expert', axis=0, tiled=True)]
    unnamed x65 -> x75, local copies, waits for them, and re-layouts: 18.7 us -> 21.5 us
where the time goes in v1:
time: 1020 us
  waiting for transfers between devices  535 us (52%)
  starting transfers between devices  286 us (28%)
  local copies, waits for them, and re-layouts  85 us (8%)
  other arithmetic  70.8 us (7%)
  matrix products  34.4 us (3%)
    ppermute x63, waiting for transfers between devices, from_behind(): return lax.ppermute(value, axis, pairs)  429 us
    ppermute x63, starting transfers between devices, from_behind(): return lax.ppermute(value, axis, pairs)  269 us
    all_to_all x1, waiting for transfers between devices, tiled_gather(): return lax.all_to_all(copies, axis, dim, dim, tiled=True)  41 us
    add x32, other arithmetic, advance(): return (pair_now[0][..., None, None] * state_now + pair_now[1], state_now)  37.4 us
    all_to_all x1, waiting for transfers between devices, shards(): lax.all_to_all(result.reshape(sender_count, item_count, model_width), 'ex...  26.3 us
    all_to_all x1, waiting for transfers between devices, shards(): lax.all_to_all(send_inputs, 'expert', split_axis=0, concat_axis=0, tiled=...  21.7 us
    unnamed x75, local copies, waits for them, and re-layouts  21.5 us
  transfers between devices with their start and end apart: 67, of which 66 were waited for; matrix products, arithmetic and copies ran while one was open for 7% of the time, Pallas kernels for 0%

profile of v1, /device:TPU:24, one launch (start us, length us, event | category | flops | bytes accessed | tf_op | source)
XLA Modules:
  0.0 1015.5 jit_solution(4399956458063102060)
XLA Ops:
  28.1 17.5 %all-to-all-done.1 = bf16[8,64,2048]{2,1,0:T(8,128)(2,1)} async-done(((bf16[8,64,2048]{2,1,0:T(8,128)(2,1)}), bf16[8,64,2048]{2,1,0:T(8,128)(2,1)}, u32[]{:S(2)}, u32[]{:S(2)}) %all-to-all-start.1) | async-done | bytes 2097184 | tf_op jit(solution)/shard_map/all_to_all | solution.py:229
  55.4 21.7 %all-to-all-done = bf16[8,64,2048]{2,1,0:T(8,128)(2,1)} async-done(((bf16[8,64,2048]{2,1,0:T(8,128)(2,1)}), bf16[8,64,2048]{2,1,0:T(8,128)(2,1)}, u32[]{:S(2)}, u32[]{:S(2)}) %all-to-all-start) | async-done | bytes 2097184 | tf_op jit(solution)/shard_map/all_to_all | solution.py:228
  77.1 7.3 fusion.12
  89.0 26.3 %all-to-all-done.2 = bf16[8,64,2048]{2,1,0:T(8,128)(2,1)S(1)} async-done(((bf16[8,64,2048]{2,1,0:T(8,128)(2,1)}), bf16[8,64,2048]{2,1,0:T(8,128)(2,1)S(1)}, u32[]{:S(2)}, u32[]{:S(2)}) %all-to-all-start.2) | async-done | bytes 2097184 | tf_op jit(solution)/shard_map/all_to_all | solution.py:239
  139.5 41.0 %all-to-all-done.3 = bf16[8,128,2048]{2,1,0:T(8,128)(2,1)} async-done(((bf16[8,128,2048]{2,1,0:T(8,128)(2,1)}), bf16[8,128,2048]{2,1,0:T(8,128)(2,1)}, u32[]{:S(2)}, u32[]{:S(2)}) %all-to-all-start.3) | async-done | bytes 4194336 | tf_op jit(solution)/shard_map/all_to_all | solution.py:14
  197.8 14.4 %while.78 = (s32[]{:T(128)}, f32[1,8,128,64]{3,2,1,0:T(8,128)S(1)}, f32[8,1,8]{2,1,0:T(1,128)}, f32[8,1,8,128,64]{4,3,2,1,0:T(8,128)}, s32[]{:T(128)}, /*index=5*/s32[]{:T(128)}, s32[]{:T(128)}) while((s32[]{:T(128)}, f32[1,8,128,64]{3,2,1,0:T(8,128)S(1)}, f32[8,1,8]{2,1,0:T(1,128)}, f32[8,1,8,128,64]{4,3,2,1,0:T(8,128)}, ...), condition=%wide.region_10.12_spmd.clone, body=%wide.region_9.11_spmd.clone.sunk | while | flops 196612 | bytes 786643 | solution.py:96
  212.3 352.8 %while.79 = (s32[]{:T(128)}, f32[1,8,128,64]{3,2,1,0:T(8,128)S(1)}, f32[1,8]{1,0:T(1,128)S(1)}, f32[1,8,128,64]{3,2,1,0:T(8,128)S(1)}, s32[]{:T(128)}, /*index=5*/s32[]{:T(128)}) while((s32[]{:T(128)}, f32[1,8,128,64]{3,2,1,0:T(8,128)S(1)}, f32[1,8]{1,0:T(1,128)S(1)}, f32[1,8,128,64]{3,2,1,0:T(8,128)S(1)}, s32[]{:T(128)}, ...), condition=%wide.region_12.14_spmd.clone, body=%wide.region_11.13_spmd.clone.sunk | while | flops 327683 | bytes 1573015 | solution.py:261
  212.4 7.9 collective-permute-start
  237.0 6.5 collective-permute-start
  258.2 6.5 collective-permute-start
  268.7 6.5 collective-permute-start
  279.3 6.5 collective-permute-start
  381.8 6.5 collective-permute-start
  567.0 20.7 %while.76 = (s32[]{:T(128)}, f32[1,8,128,64]{3,2,1,0:T(8,128)S(1)}, bf16[8,1,8,128,64]{4,3,2,1,0:T(8,128)(2,1)}, f32[8,1,8]{2,1,0:T(1,128)}, f32[8,1,8,128,64]{4,3,2,1,0:T(8,128)}, /*index=5*/s32[]{:T(128)}, s32[]{:T(128)}) while((s32[]{:T(128)}, f32[1,8,128,64]{3,2,1,0:T(8,128)S(1)}, bf16[8,1,8,128,64]{4,3,2,1,0:T(8,128)(2,1)}, ...), condition=%wide.region_14.16_spmd, body=%wide.region_13.15_spmd.sunk | while | flops 131075 | bytes 1573069 | solution.py:96
  615.8 14.4 %while.80 = (s32[]{:T(128)}, f32[1,8,128,64]{3,2,1,0:T(8,128)S(1)}, f32[8,1,8]{2,1,0:T(1,128)}, f32[8,1,8,128,64]{4,3,2,1,0:T(8,128)}, s32[]{:T(128)}, /*index=5*/s32[]{:T(128)}) while((s32[]{:T(128)}, f32[1,8,128,64]{3,2,1,0:T(8,128)S(1)}, f32[8,1,8]{2,1,0:T(1,128)}, f32[8,1,8,128,64]{4,3,2,1,0:T(8,128)}, s32[]{:T(128)}, ...), condition=%wide.region_17.19_spmd.clone, body=%wide.region_16.18_spmd.clone.sunk | while | flops 196611 | bytes 786623 | solution.py:90
  630.2 350.9 %while.81 = (s32[]{:T(128)}, f32[1,8,128,64]{3,2,1,0:T(8,128)S(1)}, f32[1,8]{1,0:T(1,128)S(1)}, f32[1,8,128,64]{3,2,1,0:T(8,128)S(1)}, s32[]{:T(128)}, /*index=5*/s32[]{:T(128)}) while((s32[]{:T(128)}, f32[1,8,128,64]{3,2,1,0:T(8,128)S(1)}, f32[1,8]{1,0:T(1,128)S(1)}, f32[1,8,128,64]{3,2,1,0:T(8,128)S(1)}, s32[]{:T(128)}, ...), condition=%wide.region_19.21_spmd.clone, body=%wide.region_18.20_spmd.clone.sunk | while | flops 327683 | bytes 1573015 | solution.py:210
  632.3 8.4 collective-permute-done.1
  642.9 9.1 collective-permute-done.1
  654.1 10.3 %collective-permute-done.1 = bf16[1,8,128,64]{3,2,1,0:T(8,128)(2,1)S(1)} collective-permute-done((bf16[1,8,128,64]{3,2,1,0:T(8,128)(2,1)S(1)}, bf16[1,8,128,64]{3,2,1,0:T(8,128)(2,1)S(1)}, u32[]{:S(2)}, u32[]{:S(2)}) %collective-permute-start.1) | collective-permute-done | bytes 131104 | tf_op jit(solution)/shard_map/while/body/eval_jaxpr/ppermute | solution.py:20
  666.5 11.1 %collective-permute-done.1 = bf16[1,8,128,64]{3,2,1,0:T(8,128)(2,1)S(1)} collective-permute-done((bf16[1,8,128,64]{3,2,1,0:T(8,128)(2,1)S(1)}, bf16[1,8,128,64]{3,2,1,0:T(8,128)(2,1)S(1)}, u32[]{:S(2)}, u32[]{:S(2)}) %collective-permute-start.1) | collective-permute-done | bytes 131104 | tf_op jit(solution)/shard_map/while/body/eval_jaxpr/ppermute | solution.py:20
  679.7 10.3 %collective-permute-done.1 = bf16[1,8,128,64]{3,2,1,0:T(8,128)(2,1)S(1)} collective-permute-done((bf16[1,8,128,64]{3,2,1,0:T(8,128)(2,1)S(1)}, bf16[1,8,128,64]{3,2,1,0:T(8,128)(2,1)S(1)}, u32[]{:S(2)}, u32[]{:S(2)}) %collective-permute-start.1) | collective-permute-done | bytes 131104 | tf_op jit(solution)/shard_map/while/body/eval_jaxpr/ppermute | solution.py:20
  692.1 9.4 collective-permute-done.1
  703.6 8.5 collective-permute-done.1
  714.2 8.4 collective-permute-done.1
  724.7 8.4 collective-permute-done.1
  735.3 8.4 collective-permute-done.1
  745.9 9.2 collective-permute-done.1
  757.2 10.3 %collective-permute-done.1 = bf16[1,8,128,64]{3,2,1,0:T(8,128)(2,1)S(1)} collective-permute-done((bf16[1,8,128,64]{3,2,1,0:T(8,128)(2,1)S(1)}, bf16[1,8,128,64]{3,2,1,0:T(8,128)(2,1)S(1)}, u32[]{:S(2)}, u32[]{:S(2)}) %collective-permute-start.1) | collective-permute-done | bytes 131104 | tf_op jit(solution)/shard_map/while/body/eval_jaxpr/ppermute | solution.py:20
  769.6 11.0 %collective-permute-done.1 = bf16[1,8,128,64]{3,2,1,0:T(8,128)(2,1)S(1)} collective-permute-done((bf16[1,8,128,64]{3,2,1,0:T(8,128)(2,1)S(1)}, bf16[1,8,128,64]{3,2,1,0:T(8,128)(2,1)S(1)}, u32[]{:S(2)}, u32[]{:S(2)}) %collective-permute-start.1) | collective-permute-done | bytes 131104 | tf_op jit(solution)/shard_map/while/body/eval_jaxpr/ppermute | solution.py:20
  782.8 10.2 %collective-permute-done.1 = bf16[1,8,128,64]{3,2,1,0:T(8,128)(2,1)S(1)} collective-permute-done((bf16[1,8,128,64]{3,2,1,0:T(8,128)(2,1)S(1)}, bf16[1,8,128,64]{3,2,1,0:T(8,128)(2,1)S(1)}, u32[]{:S(2)}, u32[]{:S(2)}) %collective-permute-start.1) | collective-permute-done | bytes 131104 | tf_op jit(solution)/shard_map/while/body/eval_jaxpr/ppermute | solution.py:20
  795.0 9.3 collective-permute-done.1
  806.5 8.4 collective-permute-done.1
  817.0 8.4 collective-permute-done.1
  827.6 8.4 collective-permute-done.1
  838.2 8.4 collective-permute-done.1
  848.7 9.2 collective-permute-done.1
  860.1 10.4 %collective-permute-done.1 = bf16[1,8,128,64]{3,2,1,0:T(8,128)(2,1)S(1)} collective-permute-done((bf16[1,8,128,64]{3,2,1,0:T(8,128)(2,1)S(1)}, bf16[1,8,128,64]{3,2,1,0:T(8,128)(2,1)S(1)}, u32[]{:S(2)}, u32[]{:S(2)}) %collective-permute-start.1) | collective-permute-done | bytes 131104 | tf_op jit(solution)/shard_map/while/body/eval_jaxpr/ppermute | solution.py:20
  872.6 11.0 %collective-permute-done.1 = bf16[1,8,128,64]{3,2,1,0:T(8,128)(2,1)S(1)} collective-permute-done((bf16[1,8,128,64]{3,2,1,0:T(8,128)(2,1)S(1)}, bf16[1,8,128,64]{3,2,1,0:T(8,128)(2,1)S(1)}, u32[]{:S(2)}, u32[]{:S(2)}) %collective-permute-start.1) | collective-permute-done | bytes 131104 | tf_op jit(solution)/shard_map/while/body/eval_jaxpr/ppermute | solution.py:20
  885.7 10.1 collective-permute-done.1
  897.9 9.2 collective-permute-done.1
  909.3 8.4 collective-permute-done.1
  919.8 8.4 collective-permute-done.1
  930.4 8.4 collective-permute-done.1
  940.9 8.4 collective-permute-done.1
  951.5 8.4 collective-permute-done.1
  962.1 8.4 collective-permute-done.1
  972.6 8.4 collective-permute-done.1
  983.0 20.6 %while.77 = (s32[]{:T(128)}, f32[1,8,128,64]{3,2,1,0:T(8,128)S(1)}, bf16[8,1,8,128,64]{4,3,2,1,0:T(8,128)(2,1)}, f32[8,1,8]{2,1,0:T(1,128)}, f32[8,1,8,128,64]{4,3,2,1,0:T(8,128)}, /*index=5*/s32[]{:T(128)}) while((s32[]{:T(128)}, f32[1,8,128,64]{3,2,1,0:T(8,128)S(1)}, bf16[8,1,8,128,64]{4,3,2,1,0:T(8,128)(2,1)}, f32[8,1,8]{2,1,0:T(1,128)}, ...), condition=%wide.region_21.23_spmd, body=%wide.region_20.22_spmd.sunk | while | flops 131074 | bytes 1573049 | solution.py:90
  (442 shorter events, 572.2 us)
Async XLA Ops:
  13.9 31.6 %all-to-all-start.1 = ((bf16[8,64,2048]{2,1,0:T(8,128)(2,1)}), bf16[8,64,2048]{2,1,0:T(8,128)(2,1)}, u32[]{:S(2)}, u32[]{:S(2)}) async-start(bf16[8,64,2048]{2,1,0:T(8,128)(2,1)} %bitcast.211), calls=%async_computation.1 | async-start | bytes 4194304 | tf_op jit(solution)/shard_map/all_to_all | solution.py:229
  45.5 31.6 %all-to-all-start = ((bf16[8,64,2048]{2,1,0:T(8,128)(2,1)}), bf16[8,64,2048]{2,1,0:T(8,128)(2,1)}, u32[]{:S(2)}, u32[]{:S(2)}) async-start(bf16[8,64,2048]{2,1,0:T(8,128)(2,1)} %bitcast.210), calls=%async_computation | async-start | bytes 4194304 | tf_op jit(solution)/shard_map/all_to_all | solution.py:228
  84.4 30.9 %all-to-all-start.2 = ((bf16[8,64,2048]{2,1,0:T(8,128)(2,1)}), bf16[8,64,2048]{2,1,0:T(8,128)(2,1)S(1)}, u32[]{:S(2)}, u32[]{:S(2)}) async-start(bf16[8,64,2048]{2,1,0:T(8,128)(2,1)} %bitcast.226), calls=%async_computation.2 | async-start | bytes 4194304 | tf_op jit(solution)/shard_map/all_to_all | solution.py:239
  126.3 54.2 %all-to-all-start.3 = ((bf16[8,128,2048]{2,1,0:T(8,128)(2,1)}), bf16[8,128,2048]{2,1,0:T(8,128)(2,1)}, u32[]{:S(2)}, u32[]{:S(2)}) async-start(bf16[8,128,2048]{2,1,0:T(8,128)(2,1)} %bitcast.212), calls=%async_computation.3 | async-start | bytes 8388608 | tf_op jit(solution)/shard_map/all_to_all | solution.py:14
  212.4 13.3 %collective-permute-start = (bf16[1,8,128,64]{3,2,1,0:T(8,128)(2,1)S(1)}, bf16[1,8,128,64]{3,2,1,0:T(8,128)(2,1)S(1)}, u32[]{:S(2)}, u32[]{:S(2)}) collective-permute-start(bf16[1,8,128,64]{3,2,1,0:T(8,128)(2,1)S(1)} %fusion.99), channel_id=1, source_target_pairs={{8,0},{16,8},{24,16},{32,24},{40,32},{48,40},{56,48},{64,56},{72,6... | collective-permute-start | bytes 393224 | tf_op jit(solution)/shard_map/while/body/eval_jaxpr/ppermute | solution.py:20
  225.9 11.0 %collective-permute-start = (bf16[1,8,128,64]{3,2,1,0:T(8,128)(2,1)S(1)}, bf16[1,8,128,64]{3,2,1,0:T(8,128)(2,1)S(1)}, u32[]{:S(2)}, u32[]{:S(2)}) collective-permute-start(bf16[1,8,128,64]{3,2,1,0:T(8,128)(2,1)S(1)} %fusion.99), channel_id=1, source_target_pairs={{8,0},{16,8},{24,16},{32,24},{40,32},{48,40},{56,48},{64,56},{72,6... | collective-permute-start | bytes 393224 | tf_op jit(solution)/shard_map/while/body/eval_jaxpr/ppermute | solution.py:20
  237.0 10.4 %collective-permute-start = (bf16[1,8,128,64]{3,2,1,0:T(8,128)(2,1)S(1)}, bf16[1,8,128,64]{3,2,1,0:T(8,128)(2,1)S(1)}, u32[]{:S(2)}, u32[]{:S(2)}) collective-permute-start(bf16[1,8,128,64]{3,2,1,0:T(8,128)(2,1)S(1)} %fusion.99), channel_id=1, source_target_pairs={{8,0},{16,8},{24,16},{32,24},{40,32},{48,40},{56,48},{64,56},{72,6... | collective-permute-start | bytes 393224 | tf_op jit(solution)/shard_map/while/body/eval_jaxpr/ppermute | solution.py:20
  247.6 10.4 %collective-permute-start = (bf16[1,8,128,64]{3,2,1,0:T(8,128)(2,1)S(1)}, bf16[1,8,128,64]{3,2,1,0:T(8,128)(2,1)S(1)}, u32[]{:S(2)}, u32[]{:S(2)}) collective-permute-start(bf16[1,8,128,64]{3,2,1,0:T(8,128)(2,1)S(1)} %fusion.99), channel_id=1, source_target_pairs={{8,0},{16,8},{24,16},{32,24},{40,32},{48,40},{56,48},{64,56},{72,6... | collective-permute-start | bytes 393224 | tf_op jit(solution)/shard_map/while/body/eval_jaxpr/ppermute | solution.py:20
  258.2 10.4 %collective-permute-start = (bf16[1,8,128,64]{3,2,1,0:T(8,128)(2,1)S(1)}, bf16[1,8,128,64]{3,2,1,0:T(8,128)(2,1)S(1)}, u32[]{:S(2)}, u32[]{:S(2)}) collective-permute-start(bf16[1,8,128,64]{3,2,1,0:T(8,128)(2,1)S(1)} %fusion.99), channel_id=1, source_target_pairs={{8,0},{16,8},{24,16},{32,24},{40,32},{48,40},{56,48},{64,56},{72,6... | collective-permute-start | bytes 393224 | tf_op jit(solution)/shard_map/while/body/eval_jaxpr/ppermute | solution.py:20
  268.7 10.4 %collective-permute-start = (bf16[1,8,128,64]{3,2,1,0:T(8,128)(2,1)S(1)}, bf16[1,8,128,64]{3,2,1,0:T(8,128)(2,1)S(1)}, u32[]{:S(2)}, u32[]{:S(2)}) collective-permute-start(bf16[1,8,128,64]{3,2,1,0:T(8,128)(2,1)S(1)} %fusion.99), channel_id=1, source_target_pairs={{8,0},{16,8},{24,16},{32,24},{40,32},{48,40},{56,48},{64,56},{72,6... | collective-permute-start | bytes 393224 | tf_op jit(solution)/shard_map/while/body/eval_jaxpr/ppermute | solution.py:20
  279.3 11.5 %collective-permute-start = (bf16[1,8,128,64]{3,2,1,0:T(8,128)(2,1)S(1)}, bf16[1,8,128,64]{3,2,1,0:T(8,128)(2,1)S(1)}, u32[]{:S(2)}, u32[]{:S(2)}) collective-permute-start(bf16[1,8,128,64]{3,2,1,0:T(8,128)(2,1)S(1)} %fusion.99), channel_id=1, source_target_pairs={{8,0},{16,8},{24,16},{32,24},{40,32},{48,40},{56,48},{64,56},{72,6... | collective-permute-start | bytes 393224 | tf_op jit(solution)/shard_map/while/body/eval_jaxpr/ppermute | solution.py:20
  291.0 12.7 %collective-permute-start = (bf16[1,8,128,64]{3,2,1,0:T(8,128)(2,1)S(1)}, bf16[1,8,128,64]{3,2,1,0:T(8,128)(2,1)S(1)}, u32[]{:S(2)}, u32[]{:S(2)}) collective-permute-start(bf16[1,8,128,64]{3,2,1,0:T(8,128)(2,1)S(1)} %fusion.99), channel_id=1, source_target_pairs={{8,0},{16,8},{24,16},{32,24},{40,32},{48,40},{56,48},{64,56},{72,6... | collective-permute-start | bytes 393224 | tf_op jit(solution)/shard_map/while/body/eval_jaxpr/ppermute | solution.py:20
  303.8 12.6 %collective-permute-start = (bf16[1,8,128,64]{3,2,1,0:T(8,128)(2,1)S(1)}, bf16[1,8,128,64]{3,2,1,0:T(8,128)(2,1)S(1)}, u32[]{:S(2)}, u32[]{:S(2)}) collective-permute-start(bf16[1,8,128,64]{3,2,1,0:T(8,128)(2,1)S(1)} %fusion.99), channel_id=1, source_target_pairs={{8,0},{16,8},{24,16},{32,24},{40,32},{48,40},{56,48},{64,56},{72,6... | collective-permute-start | bytes 393224 | tf_op jit(solution)/shard_map/while/body/eval_jaxpr/ppermute | solution.py:20
  316.6 11.8 %collective-permute-start = (bf16[1,8,128,64]{3,2,1,0:T(8,128)(2,1)S(1)}, bf16[1,8,128,64]{3,2,1,0:T(8,128)(2,1)S(1)}, u32[]{:S(2)}, u32[]{:S(2)}) collective-permute-start(bf16[1,8,128,64]{3,2,1,0:T(8,128)(2,1)S(1)} %fusion.99), channel_id=1, source_target_pairs={{8,0},{16,8},{24,16},{32,24},{40,32},{48,40},{56,48},{64,56},{72,6... | collective-permute-start | bytes 393224 | tf_op jit(solution)/shard_map/while/body/eval_jaxpr/ppermute | solution.py:20
  328.5 10.8 %collective-permute-start = (bf16[1,8,128,64]{3,2,1,0:T(8,128)(2,1)S(1)}, bf16[1,8,128,64]{3,2,1,0:T(8,128)(2,1)S(1)}, u32[]{:S(2)}, u32[]{:S(2)}) collective-permute-start(bf16[1,8,128,64]{3,2,1,0:T(8,128)(2,1)S(1)} %fusion.99), channel_id=1, source_target_pairs={{8,0},{16,8},{24,16},{32,24},{40,32},{48,40},{56,48},{64,56},{72,6... | collective-permute-start | bytes 393224 | tf_op jit(solution)/shard_map/while/body/eval_jaxpr/ppermute | solution.py:20
  339.5 10.4 %collective-permute-start = (bf16[1,8,128,64]{3,2,1,0:T(8,128)(2,1)S(1)}, bf16[1,8,128,64]{3,2,1,0:T(8,128)(2,1)S(1)}, u32[]{:S(2)}, u32[]{:S(2)}) collective-permute-start(bf16[1,8,128,64]{3,2,1,0:T(8,128)(2,1)S(1)} %fusion.99), channel_id=1, source_target_pairs={{8,0},{16,8},{24,16},{32,24},{40,32},{48,40},{56,48},{64,56},{72,6... | collective-permute-start | bytes 393224 | tf_op jit(solution)/shard_map/while/body/eval_jaxpr/ppermute | solution.py:20
  350.1 10.4 %collective-permute-start = (bf16[1,8,128,64]{3,2,1,0:T(8,128)(2,1)S(1)}, bf16[1,8,128,64]{3,2,1,0:T(8,128)(2,1)S(1)}, u32[]{:S(2)}, u32[]{:S(2)}) collective-permute-start(bf16[1,8,128,64]{3,2,1,0:T(8,128)(2,1)S(1)} %fusion.99), channel_id=1, source_target_pairs={{8,0},{16,8},{24,16},{32,24},{40,32},{48,40},{56,48},{64,56},{72,6... | collective-permute-start | bytes 393224 | tf_op jit(solution)/shard_map/while/body/eval_jaxpr/ppermute | solution.py:20
  360.7 10.4 %collective-permute-start = (bf16[1,8,128,64]{3,2,1,0:T(8,128)(2,1)S(1)}, bf16[1,8,128,64]{3,2,1,0:T(8,128)(2,1)S(1)}, u32[]{:S(2)}, u32[]{:S(2)}) collective-permute-start(bf16[1,8,128,64]{3,2,1,0:T(8,128)(2,1)S(1)} %fusion.99), channel_id=1, source_target_pairs={{8,0},{16,8},{24,16},{32,24},{40,32},{48,40},{56,48},{64,56},{72,6... | collective-permute-start | bytes 393224 | tf_op jit(solution)/shard_map/while/body/eval_jaxpr/ppermute | solution.py:20
  371.2 10.4 %collective-permute-start = (bf16[1,8,128,64]{3,2,1,0:T(8,128)(2,1)S(1)}, bf16[1,8,128,64]{3,2,1,0:T(8,128)(2,1)S(1)}, u32[]{:S(2)}, u32[]{:S(2)}) collective-permute-start(bf16[1,8,128,64]{3,2,1,0:T(8,128)(2,1)S(1)} %fusion.99), channel_id=1, source_target_pairs={{8,0},{16,8},{24,16},{32,24},{40,32},{48,40},{56,48},{64,56},{72,6... | collective-permute-start | bytes 393224 | tf_op jit(solution)/shard_map/while/body/eval_jaxpr/ppermute | solution.py:20
  381.8 11.5 %collective-permute-start = (bf16[1,8,128,64]{3,2,1,0:T(8,128)(2,1)S(1)}, bf16[1,8,128,64]{3,2,1,0:T(8,128)(2,1)S(1)}, u32[]{:S(2)}, u32[]{:S(2)}) collective-permute-start(bf16[1,8,128,64]{3,2,1,0:T(8,128)(2,1)S(1)} %fusion.99), channel_id=1, source_target_pairs={{8,0},{16,8},{24,16},{32,24},{40,32},{48,40},{56,48},{64,56},{72,6... | collective-permute-start | bytes 393224 | tf_op jit(solution)/shard_map/while/body/eval_jaxpr/ppermute | solution.py:20
  393.5 12.7 %collective-permute-start = (bf16[1,8,128,64]{3,2,1,0:T(8,128)(2,1)S(1)}, bf16[1,8,128,64]{3,2,1,0:T(8,128)(2,1)S(1)}, u32[]{:S(2)}, u32[]{:S(2)}) collective-permute-start(bf16[1,8,128,64]{3,2,1,0:T(8,128)(2,1)S(1)} %fusion.99), channel_id=1, source_target_pairs={{8,0},{16,8},{24,16},{32,24},{40,32},{48,40},{56,48},{64,56},{72,6... | collective-permute-start | bytes 393224 | tf_op jit(solution)/shard_map/while/body/eval_jaxpr/ppermute | solution.py:20
  406.4 12.5 %collective-permute-start = (bf16[1,8,128,64]{3,2,1,0:T(8,128)(2,1)S(1)}, bf16[1,8,128,64]{3,2,1,0:T(8,128)(2,1)S(1)}, u32[]{:S(2)}, u32[]{:S(2)}) collective-permute-start(bf16[1,8,128,64]{3,2,1,0:T(8,128)(2,1)S(1)} %fusion.99), channel_id=1, source_target_pairs={{8,0},{16,8},{24,16},{32,24},{40,32},{48,40},{56,48},{64,56},{72,6... | collective-permute-start | bytes 393224 | tf_op jit(solution)/shard_map/while/body/eval_jaxpr/ppermute | solution.py:20
  419.1 11.7 %collective-permute-start = (bf16[1,8,128,64]{3,2,1,0:T(8,128)(2,1)S(1)}, bf16[1,8,128,64]{3,2,1,0:T(8,128)(2,1)S(1)}, u32[]{:S(2)}, u32[]{:S(2)}) collective-permute-start(bf16[1,8,128,64]{3,2,1,0:T(8,128)(2,1)S(1)} %fusion.99), channel_id=1, source_target_pairs={{8,0},{16,8},{24,16},{32,24},{40,32},{48,40},{56,48},{64,56},{72,6... | collective-permute-start | bytes 393224 | tf_op jit(solution)/shard_map/while/body/eval_jaxpr/ppermute | solution.py:20
  431.0 10.8 %collective-permute-start = (bf16[1,8,128,64]{3,2,1,0:T(8,128)(2,1)S(1)}, bf16[1,8,128,64]{3,2,1,0:T(8,128)(2,1)S(1)}, u32[]{:S(2)}, u32[]{:S(2)}) collective-permute-start(bf16[1,8,128,64]{3,2,1,0:T(8,128)(2,1)S(1)} %fusion.99), channel_id=1, source_target_pairs={{8,0},{16,8},{24,16},{32,24},{40,32},{48,40},{56,48},{64,56},{72,6... | collective-permute-start | bytes 393224 | tf_op jit(solution)/shard_map/while/body/eval_jaxpr/ppermute | solution.py:20
  473.7 10.5 %collective-permute-start = (bf16[1,8,128,64]{3,2,1,0:T(8,128)(2,1)S(1)}, bf16[1,8,128,64]{3,2,1,0:T(8,128)(2,1)S(1)}, u32[]{:S(2)}, u32[]{:S(2)}) collective-permute-start(bf16[1,8,128,64]{3,2,1,0:T(8,128)(2,1)S(1)} %fusion.99), channel_id=1, source_target_pairs={{8,0},{16,8},{24,16},{32,24},{40,32},{48,40},{56,48},{64,56},{72,6... | collective-permute-start | bytes 393224 | tf_op jit(solution)/shard_map/while/body/eval_jaxpr/ppermute | solution.py:20
  484.4 11.5 %collective-permute-start = (bf16[1,8,128,64]{3,2,1,0:T(8,128)(2,1)S(1)}, bf16[1,8,128,64]{3,2,1,0:T(8,128)(2,1)S(1)}, u32[]{:S(2)}, u32[]{:S(2)}) collective-permute-start(bf16[1,8,128,64]{3,2,1,0:T(8,128)(2,1)S(1)} %fusion.99), channel_id=1, source_target_pairs={{8,0},{16,8},{24,16},{32,24},{40,32},{48,40},{56,48},{64,56},{72,6... | collective-permute-start | bytes 393224 | tf_op jit(solution)/shard_map/while/body/eval_jaxpr/ppermute | solution.py:20
  496.1 12.8 %collective-permute-start = (bf16[1,8,128,64]{3,2,1,0:T(8,128)(2,1)S(1)}, bf16[1,8,128,64]{3,2,1,0:T(8,128)(2,1)S(1)}, u32[]{:S(2)}, u32[]{:S(2)}) collective-permute-start(bf16[1,8,128,64]{3,2,1,0:T(8,128)(2,1)S(1)} %fusion.99), channel_id=1, source_target_pairs={{8,0},{16,8},{24,16},{32,24},{40,32},{48,40},{56,48},{64,56},{72,6... | collective-permute-start | bytes 393224 | tf_op jit(solution)/shard_map/while/body/eval_jaxpr/ppermute | solution.py:20
  509.0 12.5 %collective-permute-start = (bf16[1,8,128,64]{3,2,1,0:T(8,128)(2,1)S(1)}, bf16[1,8,128,64]{3,2,1,0:T(8,128)(2,1)S(1)}, u32[]{:S(2)}, u32[]{:S(2)}) collective-permute-start(bf16[1,8,128,64]{3,2,1,0:T(8,128)(2,1)S(1)} %fusion.99), channel_id=1, source_target_pairs={{8,0},{16,8},{24,16},{32,24},{40,32},{48,40},{56,48},{64,56},{72,6... | collective-permute-start | bytes 393224 | tf_op jit(solution)/shard_map/while/body/eval_jaxpr/ppermute | solution.py:20
  521.7 11.7 %collective-permute-start = (bf16[1,8,128,64]{3,2,1,0:T(8,128)(2,1)S(1)}, bf16[1,8,128,64]{3,2,1,0:T(8,128)(2,1)S(1)}, u32[]{:S(2)}, u32[]{:S(2)}) collective-permute-start(bf16[1,8,128,64]{3,2,1,0:T(8,128)(2,1)S(1)} %fusion.99), channel_id=1, source_target_pairs={{8,0},{16,8},{24,16},{32,24},{40,32},{48,40},{56,48},{64,56},{72,6... | collective-permute-start | bytes 393224 | tf_op jit(solution)/shard_map/while/body/eval_jaxpr/ppermute | solution.py:20
  533.5 10.4 %collective-permute-start = (bf16[1,8,128,64]{3,2,1,0:T(8,128)(2,1)S(1)}, bf16[1,8,128,64]{3,2,1,0:T(8,128)(2,1)S(1)}, u32[]{:S(2)}, u32[]{:S(2)}) collective-permute-start(bf16[1,8,128,64]{3,2,1,0:T(8,128)(2,1)S(1)} %fusion.99), channel_id=1, source_target_pairs={{8,0},{16,8},{24,16},{32,24},{40,32},{48,40},{56,48},{64,56},{72,6... | collective-permute-start | bytes 393224 | tf_op jit(solution)/shard_map/while/body/eval_jaxpr/ppermute | solution.py:20
  544.1 10.4 %collective-permute-start = (bf16[1,8,128,64]{3,2,1,0:T(8,128)(2,1)S(1)}, bf16[1,8,128,64]{3,2,1,0:T(8,128)(2,1)S(1)}, u32[]{:S(2)}, u32[]{:S(2)}) collective-permute-start(bf16[1,8,128,64]{3,2,1,0:T(8,128)(2,1)S(1)} %fusion.99), channel_id=1, source_target_pairs={{8,0},{16,8},{24,16},{32,24},{40,32},{48,40},{56,48},{64,56},{72,6... | collective-permute-start | bytes 393224 | tf_op jit(solution)/shard_map/while/body/eval_jaxpr/ppermute | solution.py:20
  605.5 402.6 %collective-permute-start.2 = (f32[3,512]{0,1:T(8,128)}, f32[3,512]{0,1:T(8,128)}, u32[]{:S(2)}, u32[]{:S(2)}) collective-permute-start(f32[3,512]{0,1:T(8,128)} %slice.54), channel_id=1, source_target_pairs={{8,0},{16,8},{24,16},{32,24},{40,32},{48,40},{56,48},{64,56},{72,6... | collective-permute-start | bytes 18440 | tf_op jit(solution)/shard_map/ppermute | solution.py:20
  640.9 11.0 %collective-permute-start.1 = (bf16[1,8,128,64]{3,2,1,0:T(8,128)(2,1)S(1)}, bf16[1,8,128,64]{3,2,1,0:T(8,128)(2,1)S(1)}, u32[]{:S(2)}, u32[]{:S(2)}) collective-permute-start(bf16[1,8,128,64]{3,2,1,0:T(8,128)(2,1)S(1)} %fusion.100), channel_id=1, source_target_pairs={{0,8},{8,16},{16,24},{24,32},{32,40},{40,48},{48,56},{56,64},{64,7... | collective-permute-start | bytes 393224 | tf_op jit(solution)/shard_map/while/body/eval_jaxpr/ppermute | solution.py:20
  652.1 12.2 %collective-permute-start.1 = (bf16[1,8,128,64]{3,2,1,0:T(8,128)(2,1)S(1)}, bf16[1,8,128,64]{3,2,1,0:T(8,128)(2,1)S(1)}, u32[]{:S(2)}, u32[]{:S(2)}) collective-permute-start(bf16[1,8,128,64]{3,2,1,0:T(8,128)(2,1)S(1)} %fusion.100), channel_id=1, source_target_pairs={{0,8},{8,16},{16,24},{24,32},{32,40},{40,48},{48,56},{56,64},{64,7... | collective-permute-start | bytes 393224 | tf_op jit(solution)/shard_map/while/body/eval_jaxpr/ppermute | solution.py:20
  664.5 13.0 %collective-permute-start.1 = (bf16[1,8,128,64]{3,2,1,0:T(8,128)(2,1)S(1)}, bf16[1,8,128,64]{3,2,1,0:T(8,128)(2,1)S(1)}, u32[]{:S(2)}, u32[]{:S(2)}) collective-permute-start(bf16[1,8,128,64]{3,2,1,0:T(8,128)(2,1)S(1)} %fusion.100), channel_id=1, source_target_pairs={{0,8},{8,16},{16,24},{24,32},{32,40},{40,48},{48,56},{56,64},{64,7... | collective-permute-start | bytes 393224 | tf_op jit(solution)/shard_map/while/body/eval_jaxpr/ppermute | solution.py:20
  677.8 12.2 %collective-permute-start.1 = (bf16[1,8,128,64]{3,2,1,0:T(8,128)(2,1)S(1)}, bf16[1,8,128,64]{3,2,1,0:T(8,128)(2,1)S(1)}, u32[]{:S(2)}, u32[]{:S(2)}) collective-permute-start(bf16[1,8,128,64]{3,2,1,0:T(8,128)(2,1)S(1)} %fusion.100), channel_id=1, source_target_pairs={{0,8},{8,16},{16,24},{24,32},{32,40},{40,48},{48,56},{56,64},{64,7... | collective-permute-start | bytes 393224 | tf_op jit(solution)/shard_map/while/body/eval_jaxpr/ppermute | solution.py:20
  690.1 11.3 %collective-permute-start.1 = (bf16[1,8,128,64]{3,2,1,0:T(8,128)(2,1)S(1)}, bf16[1,8,128,64]{3,2,1,0:T(8,128)(2,1)S(1)}, u32[]{:S(2)}, u32[]{:S(2)}) collective-permute-start(bf16[1,8,128,64]{3,2,1,0:T(8,128)(2,1)S(1)} %fusion.100), channel_id=1, source_target_pairs={{0,8},{8,16},{16,24},{24,32},{32,40},{40,48},{48,56},{56,64},{64,7... | collective-permute-start | bytes 393224 | tf_op jit(solution)/shard_map/while/body/eval_jaxpr/ppermute | solution.py:20
  701.6 10.4 %collective-permute-start.1 = (bf16[1,8,128,64]{3,2,1,0:T(8,128)(2,1)S(1)}, bf16[1,8,128,64]{3,2,1,0:T(8,128)(2,1)S(1)}, u32[]{:S(2)}, u32[]{:S(2)}) collective-permute-start(bf16[1,8,128,64]{3,2,1,0:T(8,128)(2,1)S(1)} %fusion.100), channel_id=1, source_target_pairs={{0,8},{8,16},{16,24},{24,32},{32,40},{40,48},{48,56},{56,64},{64,7... | collective-permute-start | bytes 393224 | tf_op jit(solution)/shard_map/while/body/eval_jaxpr/ppermute | solution.py:20
  743.9 11.1 %collective-permute-start.1 = (bf16[1,8,128,64]{3,2,1,0:T(8,128)(2,1)S(1)}, bf16[1,8,128,64]{3,2,1,0:T(8,128)(2,1)S(1)}, u32[]{:S(2)}, u32[]{:S(2)}) collective-permute-start(bf16[1,8,128,64]{3,2,1,0:T(8,128)(2,1)S(1)} %fusion.100), channel_id=1, source_target_pairs={{0,8},{8,16},{16,24},{24,32},{32,40},{40,48},{48,56},{56,64},{64,7... | collective-permute-start | bytes 393224 | tf_op jit(solution)/shard_map/while/body/eval_jaxpr/ppermute | solution.py:20
  755.2 12.3 %collective-permute-start.1 = (bf16[1,8,128,64]{3,2,1,0:T(8,128)(2,1)S(1)}, bf16[1,8,128,64]{3,2,1,0:T(8,128)(2,1)S(1)}, u32[]{:S(2)}, u32[]{:S(2)}) collective-permute-start(bf16[1,8,128,64]{3,2,1,0:T(8,128)(2,1)S(1)} %fusion.100), channel_id=1, source_target_pairs={{0,8},{8,16},{16,24},{24,32},{32,40},{40,48},{48,56},{56,64},{64,7... | collective-permute-start | bytes 393224 | tf_op jit(solution)/shard_map/while/body/eval_jaxpr/ppermute | solution.py:20
  767.7 13.0 %collective-permute-start.1 = (bf16[1,8,128,64]{3,2,1,0:T(8,128)(2,1)S(1)}, bf16[1,8,128,64]{3,2,1,0:T(8,128)(2,1)S(1)}, u32[]{:S(2)}, u32[]{:S(2)}) collective-permute-start(bf16[1,8,128,64]{3,2,1,0:T(8,128)(2,1)S(1)} %fusion.100), channel_id=1, source_target_pairs={{0,8},{8,16},{16,24},{24,32},{32,40},{40,48},{48,56},{56,64},{64,7... | collective-permute-start | bytes 393224 | tf_op jit(solution)/shard_map/while/body/eval_jaxpr/ppermute | solution.py:20
  780.8 12.1 %collective-permute-start.1 = (bf16[1,8,128,64]{3,2,1,0:T(8,128)(2,1)S(1)}, bf16[1,8,128,64]{3,2,1,0:T(8,128)(2,1)S(1)}, u32[]{:S(2)}, u32[]{:S(2)}) collective-permute-start(bf16[1,8,128,64]{3,2,1,0:T(8,128)(2,1)S(1)} %fusion.100), channel_id=1, source_target_pairs={{0,8},{8,16},{16,24},{24,32},{32,40},{40,48},{48,56},{56,64},{64,7... | collective-permute-start | bytes 393224 | tf_op jit(solution)/shard_map/while/body/eval_jaxpr/ppermute | solution.py:20
  793.1 11.2 %collective-permute-start.1 = (bf16[1,8,128,64]{3,2,1,0:T(8,128)(2,1)S(1)}, bf16[1,8,128,64]{3,2,1,0:T(8,128)(2,1)S(1)}, u32[]{:S(2)}, u32[]{:S(2)}) collective-permute-start(bf16[1,8,128,64]{3,2,1,0:T(8,128)(2,1)S(1)} %fusion.100), channel_id=1, source_target_pairs={{0,8},{8,16},{16,24},{24,32},{32,40},{40,48},{48,56},{56,64},{64,7... | collective-permute-start | bytes 393224 | tf_op jit(solution)/shard_map/while/body/eval_jaxpr/ppermute | solution.py:20
  846.8 11.2 %collective-permute-start.1 = (bf16[1,8,128,64]{3,2,1,0:T(8,128)(2,1)S(1)}, bf16[1,8,128,64]{3,2,1,0:T(8,128)(2,1)S(1)}, u32[]{:S(2)}, u32[]{:S(2)}) collective-permute-start(bf16[1,8,128,64]{3,2,1,0:T(8,128)(2,1)S(1)} %fusion.100), channel_id=1, source_target_pairs={{0,8},{8,16},{16,24},{24,32},{32,40},{40,48},{48,56},{56,64},{64,7... | collective-permute-start | bytes 393224 | tf_op jit(solution)/shard_map/while/body/eval_jaxpr/ppermute | solution.py:20
  858.2 12.3 %collective-permute-start.1 = (bf16[1,8,128,64]{3,2,1,0:T(8,128)(2,1)S(1)}, bf16[1,8,128,64]{3,2,1,0:T(8,128)(2,1)S(1)}, u32[]{:S(2)}, u32[]{:S(2)}) collective-permute-start(bf16[1,8,128,64]{3,2,1,0:T(8,128)(2,1)S(1)} %fusion.100), channel_id=1, source_target_pairs={{0,8},{8,16},{16,24},{24,32},{32,40},{40,48},{48,56},{56,64},{64,7... | collective-permute-start | bytes 393224 | tf_op jit(solution)/shard_map/while/body/eval_jaxpr/ppermute | solution.py:20
  870.7 12.9 %collective-permute-start.1 = (bf16[1,8,128,64]{3,2,1,0:T(8,128)(2,1)S(1)}, bf16[1,8,128,64]{3,2,1,0:T(8,128)(2,1)S(1)}, u32[]{:S(2)}, u32[]{:S(2)}) collective-permute-start(bf16[1,8,128,64]{3,2,1,0:T(8,128)(2,1)S(1)} %fusion.100), channel_id=1, source_target_pairs={{0,8},{8,16},{16,24},{24,32},{32,40},{40,48},{48,56},{56,64},{64,7... | collective-permute-start | bytes 393224 | tf_op jit(solution)/shard_map/while/body/eval_jaxpr/ppermute | solution.py:20
  883.8 12.0 %collective-permute-start.1 = (bf16[1,8,128,64]{3,2,1,0:T(8,128)(2,1)S(1)}, bf16[1,8,128,64]{3,2,1,0:T(8,128)(2,1)S(1)}, u32[]{:S(2)}, u32[]{:S(2)}) collective-permute-start(bf16[1,8,128,64]{3,2,1,0:T(8,128)(2,1)S(1)} %fusion.100), channel_id=1, source_target_pairs={{0,8},{8,16},{16,24},{24,32},{32,40},{40,48},{48,56},{56,64},{64,7... | collective-permute-start | bytes 393224 | tf_op jit(solution)/shard_map/while/body/eval_jaxpr/ppermute | solution.py:20
  896.0 11.1 %collective-permute-start.1 = (bf16[1,8,128,64]{3,2,1,0:T(8,128)(2,1)S(1)}, bf16[1,8,128,64]{3,2,1,0:T(8,128)(2,1)S(1)}, u32[]{:S(2)}, u32[]{:S(2)}) collective-permute-start(bf16[1,8,128,64]{3,2,1,0:T(8,128)(2,1)S(1)} %fusion.100), channel_id=1, source_target_pairs={{0,8},{8,16},{16,24},{24,32},{32,40},{40,48},{48,56},{56,64},{64,7... | collective-permute-start | bytes 393224 | tf_op jit(solution)/shard_map/while/body/eval_jaxpr/ppermute | solution.py:20
  (49 other events, 392.4 us)
